TPU v7x, 256 devices: a whole 4x4x8 slice. The times are simulated.
256 devices in a mesh: gx: 32 (over y, z), gy: 8 (over x, core).
Axes of the slice: x: 4, y: 4, z: 8, core: 2. Of those that a mesh axis runs over, the one named last changes fastest.
Arguments:
- features: bfloat16 [2048, 64, 512], P(('gx', 'gy')), may hold values from -6 to 6
- neighbours: int32 [2048, 6], P(('gx', 'gy')), may hold values from 0 to 16, as said below
- counts: int32 [256], P(('gx', 'gy')), may hold values from 1 to 8, as said below
- conv_weight: bfloat16 [64, 448], replicated, may hold values from -0.25 to 0.25
- down_weight: bfloat16 [128, 512], replicated, may hold values from -0.25 to 0.25
- head_weight: bfloat16 [128, 128], replicated, may hold values from -0.5 to 0.5
- coarse_map: int32 [256, 8], P(('gx', 'gy')), may hold values from 0 to 32, as said below
- latent_grad: bfloat16 [256, 512, 128], P(('gx', 'gy')), may hold values from -6 to 6
Outputs:
- latent: bfloat16 [256, 512, 128], P(('gx', 'gy'))
- features_grad: bfloat16 [2048, 64, 512], P(('gx', 'gy'))
- conv_grad: float32 [64, 448], replicated
- down_grad: float32 [128, 512], replicated
- head_grad: float32 [128, 128], replicated
Inputs may be any that keep to these rules, and one draw needn't show every extreme that they name: `counts`: in every draw, max(1, (devices along gx times devices along gy) // 8) columns have exactly 8 active blocks; each other column has between 1 and 4. 16 means no neighbour; a value below 8 is an active slot of the same column; a value v of 8 or more is the active slot v - 8 of the adjacent column in that direction; the z directions never name another column; inactive slots have no neighbours. `coarse_map`: 32 marks an empty octant; every other entry names an active block's octant, and each such octant is named at most once among the four columns that share a merged list.
All inputs are finite; a program needn't handle non-finite values.
Results may differ from a plain program's by a relative error of at most 0.013.
Values may be sent and summed in bfloat16 or wider, within the bound.
A program may use at most 128 MiB of HBM per device.

v0:
```python
import jax
import jax.numpy as jnp
from jax import lax
from jax.sharding import PartitionSpec as P


def from_partner(block, axis, distance):
    count = lax.axis_size(axis)
    route = []
    for low in range(count):
        high = low | 1 << distance
        if high != low and high < count:
            route += [(low, high), (high, low)]
    return lax.ppermute(block, axis, route)


def padded(block, sides, width):
    for axis, dim in sides:
        count = lax.axis_size(axis)
        forward = [(i, i + 1) for i in range(count - 1)]
        backward = [(target, source) for source, target in forward]
        low = lax.ppermute(
            lax.slice_in_dim(block, block.shape[dim] - width, None, axis=dim), axis, forward
        )
        high = lax.ppermute(lax.slice_in_dim(block, 0, width, axis=dim), axis, backward)
        block = jnp.concatenate([low, block, high], axis=dim)
    return block


def silu_grad(values):
    sigmoid_value = jax.nn.sigmoid(values)
    return sigmoid_value * (1.0 + values * (1.0 - sigmoid_value))


def octet(volume):
    return volume.reshape(volume.shape[0], volume.shape[1], 2, 2, 2, 4, 4, 4)


def face_of(cube, axis_number, upper):
    number, channels = (cube.shape[0], cube.shape[1])
    plane = lax.index_in_dim(cube, 3 if upper else 0, 5 + axis_number, keepdims=False)
    plane = lax.index_in_dim(plane, 1 if upper else 0, 2 + axis_number, keepdims=False)
    return plane.reshape(number, channels * 64)


def face_index(axis_number, upper):
    index = [slice(None)] * 8
    index[2 + axis_number] = 1 if upper else 0
    index[5 + axis_number] = 3 if upper else 0
    return tuple(index)


def expand_plane(rows, cube, axis_number):
    number, channels = (cube.shape[0], cube.shape[1])
    return jnp.expand_dims(
        rows.reshape(number, channels, 2, 2, 4, 4), (2 + axis_number, 5 + axis_number)
    )


def shift_minus(cube, rows, axis_number):
    parity, place = (2 + axis_number, 5 + axis_number)
    plane = expand_plane(rows, cube, axis_number)
    lower = lax.slice_in_dim(cube, 0, 1, axis=parity)
    upper = lax.slice_in_dim(cube, 1, 2, axis=parity)
    out_low = jnp.concatenate([plane, lax.slice_in_dim(upper, 0, 3, axis=place)], axis=place)
    return jnp.concatenate([out_low, lower], axis=parity)


def shift_plus(cube, rows, axis_number):
    parity, place = (2 + axis_number, 5 + axis_number)
    plane = expand_plane(rows, cube, axis_number)
    lower = lax.slice_in_dim(cube, 0, 1, axis=parity)
    upper = lax.slice_in_dim(cube, 1, 2, axis=parity)
    out_high = jnp.concatenate([lax.slice_in_dim(lower, 1, 4, axis=place), plane], axis=place)
    return jnp.concatenate([upper, out_high], axis=parity)


def minus_back(grad_out, axis_number):
    parity, place = (2 + axis_number, 5 + axis_number)
    grad_low = lax.slice_in_dim(grad_out, 0, 1, axis=parity)
    grad_high = lax.slice_in_dim(grad_out, 1, 2, axis=parity)
    moved = jnp.concatenate(
        [
            lax.slice_in_dim(grad_low, 1, 4, axis=place),
            jnp.zeros_like(lax.slice_in_dim(grad_low, 0, 1, axis=place)),
        ],
        axis=place,
    )
    plane = lax.index_in_dim(
        lax.index_in_dim(grad_low, 0, place, keepdims=False), 0, parity, keepdims=False
    )
    return (jnp.concatenate([grad_high, moved], axis=parity), plane)


def plus_back(grad_out, axis_number):
    parity, place = (2 + axis_number, 5 + axis_number)
    grad_low = lax.slice_in_dim(grad_out, 0, 1, axis=parity)
    grad_high = lax.slice_in_dim(grad_out, 1, 2, axis=parity)
    moved = jnp.concatenate(
        [
            jnp.zeros_like(lax.slice_in_dim(grad_high, 0, 1, axis=place)),
            lax.slice_in_dim(grad_high, 0, 3, axis=place),
        ],
        axis=place,
    )
    plane = lax.index_in_dim(
        lax.index_in_dim(grad_high, 3, place, keepdims=False), 0, parity, keepdims=False
    )
    return (jnp.concatenate([moved, grad_low], axis=parity), plane)


def face_layers(cube):
    return (
        face_of(cube, 0, True),
        face_of(cube, 0, False),
        face_of(cube, 1, True),
        face_of(cube, 1, False),
        face_of(cube, 2, True),
        face_of(cube, 2, False),
    )


def pick_rows(local_rows, remote_rows, index):
    width = local_rows.shape[1]
    pooled = jnp.concatenate(
        [local_rows, remote_rows, jnp.zeros((1, width), local_rows.dtype)], axis=0
    )
    return pooled[index]


def neighbour_stack(cube, faces, remotes, links):
    number, channels = (cube.shape[0], cube.shape[1])
    blank = jnp.zeros_like(faces[4])
    sources = (remotes[0], remotes[1], remotes[2], remotes[3], blank, blank)
    picked = [
        pick_rows(faces[direction], sources[direction], links[:, direction])
        for direction in range(6)
    ]
    fields = [
        cube,
        shift_minus(cube, picked[0], 0),
        shift_plus(cube, picked[1], 0),
        shift_minus(cube, picked[2], 1),
        shift_plus(cube, picked[3], 1),
        shift_minus(cube, picked[4], 2),
        shift_plus(cube, picked[5], 2),
    ]
    return jnp.stack(fields, axis=1).reshape(number, 7 * channels, 512)


def stack_grad(taps_grad, links):
    number, channels = (taps_grad.shape[0], taps_grad.shape[1] // 7)
    parts = taps_grad.reshape(number, 7, channels, 2, 2, 2, 4, 4, 4)
    grad_cube = parts[:, 0]
    face_grads = []
    for direction in range(6):
        axis_number = direction // 2
        if direction % 2 == 0:
            moved, plane = minus_back(parts[:, direction + 1], axis_number)
        else:
            moved, plane = plus_back(parts[:, direction + 1], axis_number)
        grad_cube = grad_cube + moved
        face_grads.append(plane.reshape(number, channels * 64))
    pools = [
        jnp.zeros((2 * number + 1, channels * 64), jnp.float32)
        .at[links[:, direction]]
        .add(face_grads[direction])
        for direction in range(6)
    ]
    for direction in range(6):
        shaped = pools[direction][:number].reshape(number, channels, 2, 2, 4, 4)
        grad_cube = grad_cube.at[face_index(direction // 2, direction % 2 == 0)].add(shaped)
    far_rows = [
        pools[direction][number : 2 * number].astype(jnp.bfloat16) for direction in range(4)
    ]
    return (grad_cube, far_rows)


def add_faces(grad_cube, into_xhigh, into_xlow, into_yhigh, into_ylow):
    number, channels = (grad_cube.shape[0], grad_cube.shape[1])

    def planes(rows):
        return rows.astype(jnp.float32).reshape(number, channels, 2, 2, 4, 4)

    grad_cube = grad_cube.at[face_index(0, True)].add(planes(into_xhigh))
    grad_cube = grad_cube.at[face_index(0, False)].add(planes(into_xlow))
    grad_cube = grad_cube.at[face_index(1, True)].add(planes(into_yhigh))
    grad_cube = grad_cube.at[face_index(1, False)].add(planes(into_ylow))
    return grad_cube


def merge_pool(own_rows):
    beside_y = from_partner(own_rows, "gy", 0)
    received = from_partner(jnp.concatenate([own_rows, beside_y], axis=0), "gx", 0)
    half = own_rows.shape[0]
    return jnp.concatenate([own_rows, received[:half], beside_y, received[half:]], axis=0)


def split_pool(back_rows):
    half = back_rows.shape[0] // 4
    own_part = back_rows[:half].astype(jnp.float32)
    along_x = back_rows[half : 2 * half]
    along_y = back_rows[2 * half : 3 * half]
    diagonal = back_rows[3 * half :]
    returned = from_partner(jnp.concatenate([along_x, diagonal], axis=0), "gx", 0)
    kept = own_part + returned[:half].astype(jnp.float32)
    beside = (along_y.astype(jnp.float32) + returned[half:].astype(jnp.float32)).astype(
        jnp.bfloat16
    )
    final_rows = kept + from_partner(beside, "gy", 0).astype(jnp.float32)
    return final_rows.astype(jnp.bfloat16)


def scatter_rows(volume, links, number):
    width = volume.shape[1] * volume.shape[2] // 8
    rows = volume.reshape(volume.shape[0] * 8, width)
    total = (
        jnp.zeros((4 * number + 1, width), jnp.float32)
        .at[links.reshape(-1)]
        .add(rows.astype(jnp.float32))
    )
    return total[: 4 * number].astype(jnp.bfloat16)


def body(
    features, neighbours, counts, conv_weight, down_weight, head_weight, coarse_map, latent_grad
):
    number, channels = (features.shape[0], features.shape[1])
    wide = down_weight.shape[0]
    coarse_count = coarse_map.shape[0]
    active = jnp.arange(number) < counts[0]
    masked = jnp.where(active[:, None, None], features, jnp.zeros((), jnp.bfloat16))
    cube = octet(masked)
    faces = face_layers(cube)
    rim_x = padded(jnp.stack([faces[1], faces[0]]), (("gx", 0),), 1)
    rim_y = padded(jnp.stack([faces[3], faces[2]]), (("gy", 0),), 1)
    taps = neighbour_stack(cube, faces, (rim_x[0], rim_x[3], rim_y[0], rim_y[3]), neighbours)
    hidden = jnp.einsum("ok,bkv->bov", conv_weight, taps, preferred_element_type=jnp.float32)
    act = jax.nn.silu(hidden).astype(jnp.bfloat16)
    patches = act.reshape(number, channels * 8, 64)
    octants = jnp.einsum(
        "ok,bkv->bvo", down_weight, patches, preferred_element_type=jnp.float32
    ).astype(jnp.bfloat16)
    empty_row = jnp.zeros((1, 64 * wide), jnp.bfloat16)
    merged = merge_pool(octants.reshape(number, 64 * wide))
    coarse = jnp.concatenate([merged, empty_row], axis=0)[coarse_map].reshape(
        coarse_count, 512, wide
    )
    coarse_act = jax.nn.silu(coarse.astype(jnp.float32)).astype(jnp.bfloat16)
    latent = jnp.einsum(
        "oi,cvi->cvo", head_weight, coarse_act, preferred_element_type=jnp.float32
    ).astype(jnp.bfloat16)
    act_grad = jnp.einsum(
        "oi,cvo->cvi", head_weight, latent_grad, preferred_element_type=jnp.float32
    )
    coarse_grad = (act_grad * silu_grad(coarse.astype(jnp.float32))).astype(jnp.bfloat16)
    head_part = jnp.einsum(
        "cvo,cvi->oi", latent_grad, coarse_act, preferred_element_type=jnp.float32
    )
    octant_grad = split_pool(scatter_rows(coarse_grad, coarse_map, number)).reshape(
        number, 64, wide
    )
    down_part = jnp.einsum("bvo,bkv->ok", octant_grad, patches, preferred_element_type=jnp.float32)
    patch_grad = jnp.einsum(
        "ok,bvo->bkv", down_weight, octant_grad, preferred_element_type=jnp.float32
    )
    hidden_grad = (patch_grad.reshape(number, channels, 512) * silu_grad(hidden)).astype(
        jnp.bfloat16
    )
    conv_part = jnp.einsum("bov,bkv->ok", hidden_grad, taps, preferred_element_type=jnp.float32)
    taps_grad = jnp.einsum(
        "ok,bov->bkv", conv_weight, hidden_grad, preferred_element_type=jnp.float32
    )
    near_grad, far_rows = stack_grad(taps_grad, neighbours)
    return_x = padded(jnp.stack([far_rows[0], far_rows[1]]), (("gx", 0),), 1)
    return_y = padded(jnp.stack([far_rows[2], far_rows[3]]), (("gy", 0),), 1)
    total_grad = add_faces(near_grad, return_x[3], return_x[0], return_y[3], return_y[0]).reshape(
        number, channels, 512
    )
    features_grad = jnp.where(active[:, None, None], total_grad, 0.0).astype(jnp.bfloat16)
    summed = lax.psum((conv_part, down_part, head_part), ("gx", "gy"))
    scale = float(number * lax.axis_size("gx") * lax.axis_size("gy")) ** (-0.5)
    return (latent, features_grad, summed[0] * scale, summed[1] * scale, summed[2] * scale)


def solution(mesh):
    placed = (
        P(("gx", "gy"), None, None),
        P(("gx", "gy"), None),
        P(("gx", "gy")),
        P(),
        P(),
        P(),
        P(("gx", "gy"), None),
        P(("gx", "gy"), None, None),
    )
    return jax.shard_map(
        body,
        mesh=mesh,
        in_specs=placed,
        out_specs=(P(("gx", "gy"), None, None), P(("gx", "gy"), None, None), P(), P(), P()),
        check_vma=False,
    )
```

profile of v0, /device:TPU:1, one launch (start us, length us, event | category | flops | bytes accessed | tf_op | source)
XLA Modules:
  0.0 611.4 jit_solution(5561831385059505792)
XLA Ops:
  12.5 5.0 collective-permute-start
  27.4 3.9 collective-permute-start.2
  91.6 11.2 %copy.151 = bf16[8,7,64,2,2,2,4,4,4]{2,1,8,7,6,5,4,3,0:T(8,128)(2,1)} copy(bf16[8,7,64,2,2,2,4,4,4]{2,0,8,7,6,5,4,3,1:T(8,128)(2,1)} %fusion.16) | data formatting | bytes 7340032 | tf_op jit(solution)/shard_map/stack | solution.py:148
  102.9 11.6 %reshape.747 = bf16[8,448,512]{1,2,0:T(8,128)(2,1)} reshape(bf16[8,7,64,2,2,2,4,4,4]{2,1,8,7,6,5,4,3,0:T(8,128)(2,1)} %copy.151) | data formatting | bytes 7340032 | tf_op jit(solution)/shard_map/reshape | solution.py:148
  114.5 4.6 multiply_convert_fusion.1
  124.2 6.5 %collective-permute-done.5 = bf16[16,8192]{1,0:T(8,128)(2,1)S(1)} collective-permute-done((bf16[16,8192]{1,0:T(8,128)(2,1)S(1)}, bf16[16,8192]{1,0:T(8,128)(2,1)S(1)}, u32[]{:S(2)}, u32[]{:S(2)}) %collective-permute-start.5) | collective-permute-done | bytes 262176 | tf_op jit(solution)/shard_map/ppermute | solution.py:14
  136.6 4.1 collective-permute-done.6
  149.8 3.7 convolution_bitcast_fusion.4
  153.6 4.1 convolution_bitcast_fusion
  157.6 8.8 %copy.155 = f32[8,448,512]{1,2,0:T(8,128)} copy(f32[8,448,512]{2,1,0:T(8,128)} %convolution_bitcast_fusion) | data formatting | bytes 14680064 | tf_op jit(solution)/shard_map/ok,bov->bkv/transpose | solution.py:271
  166.5 13.2 %reshape.754 = f32[8,7,64,2,2,2,4,4,4]{2,1,8,7,6,5,4,3,0:T(8,128)} reshape(f32[8,448,512]{1,2,0:T(8,128)} %copy.155) | data formatting | bytes 14680064 | tf_op jit(solution)/shard_map/reshape | solution.py:153
  179.7 53.0 %fusion.67 = (f32[8,1,64,2,2,2,4,4,4]{2,1,8,7,6,5,4,3,0:T(1,128)S(1)}, f32[8,1,64,2,2,2,4,4,4]{2,1,8,7,6,5,4,3,0:T(1,128)S(1)}, f32[8,1,64,2,2,2,4,4,4]{2,1,8,7,...) fusion(f32[8,7,64,2,2,2,4,4,4]{2,1,8,7,6,5,4,3,0:T(8,128)} %res, ...), kind=kLoop, calls=%fused_computation.173 | loop fusion | bytes 14680064 | tf_op jit(solution)/shard_map/slice | solution.py:159
  250.4 3.1 copy.166
  255.8 3.2 copy.170
  261.2 3.2 copy.162
  268.1 3.1 copy.174
  275.0 3.1 copy.178
  281.3 3.1 copy.182
  287.6 3.7 collective-permute-start.9
  295.1 3.3 collective-permute-start.11
  315.7 6.5 %fusion = f32[8,64,2,2,2,4,4,4]{1,7,6,5,4,3,2,0:T(4,128)S(1)} fusion(f32[8,64,2,2,1,4,4,3]{1,7,6,5,4,3,2,0:T(4,128)} %slice.902, f32[8,64,2,2,1,4,4,3]{1,7,6,5,4,3,2,0:T(4,128)} %slice.900, f32[8,64,2,1,2,4,3,4]{1,7,6,5,4,3,2,0:T(4,128)} %slice.896, f32[8,64,2,1,2,4,3,4]{1,7,6,5,4,3,2,0:T(4,128)} %slice.894, f32[8,64,1,2,2,3,4,4]{1,7,6,5,4,3,2,0:T(4,128)} %slice.890, ...), kind=kLoop, calls=%fused_computation.16 | loop fusion | flops 6291456 | bytes 7602176 | tf_op jit(solution)/shard_map/add | solution.py:162
  324.4 6.4 %scatter-add.109 = f32[8,64,2,2,2,4,4,4]{1,7,6,5,4,3,2,0:T(4,128)S(1)} dynamic-update-slice(f32[8,64,2,2,2,4,4,4]{1,7,6,5,4,3,2,0:T(4,128)S(1)} %fusion.23, f32[8,64,2,2,1,4,4,1]{1,7,6,5,4,3,2,0:T(1,128)} %slice_add_fusion.5, s32[]{:T(128)} %constant.277.clone.1, s32[]{:T(128)} %constant.277.clone.1, s32[]{:T(128)} %constant.277.clone.1, s32[]{:T(128)} %constant.277.clone.1, s32[]{:T(128)} %constant.282.clone.1, ...) | dynamic-update-slice | bytes 262148 | tf_op jit(solution)/shard_map/scatter-add | solution.py:172
  333.9 6.4 %scatter-add.111 = f32[8,64,2,2,2,4,4,4]{1,7,6,5,4,3,2,0:T(4,128)S(1)} dynamic-update-slice(f32[8,64,2,2,2,4,4,4]{1,7,6,5,4,3,2,0:T(4,128)S(1)} %scatter-add.109, f32[8,64,2,2,1,4,4,1]{1,7,6,5,4,3,2,0:T(1,128)} %slice_add_fusion.4, s32[]{:T(128)} %constant.277.clone.1, s32[]{:T(128)} %constant.277.clone.1, s32[]{:T(128)} %constant.277.clone.1, s32[]{:T(128)} %constant.277.clone.1, ...) | dynamic-update-slice | bytes 262148 | tf_op jit(solution)/shard_map/scatter-add | solution.py:172
  363.9 235.4 %all-reduce.9.cloned.1.call-done = (f32[64,448]{1,0:T(8,128)}, f32[128,512]{1,0:T(8,128)}, f32[128,128]{0,1:T(8,128)}) async-done(((f32[64,448]{1,0:T(8,128)}, f32[128,512]{1,0:T(8,128)}, f32[128,128]{0,1:T(8,128)}), (f32[64,448]{1,0:T(8,128)}, f32[128,512]{1,0:T(8,128)}, f32[128,128]{0,1:T(8,128)})) %all-reduce.9.cloned.1.call-update) | async-done | bytes 442384 | tf_op jit(solution)/shard_map/psum | solution.py:281
  (295 shorter events, 185.1 us)
Async XLA Ops:
  7.2 112.4 %copy-start = (bf16[128,512]{1,0:T(8,128)(2,1)S(1)}, bf16[128,512]{1,0:T(8,128)(2,1)}, u32[]{:S(2)}) copy-start(bf16[128,512]{1,0:T(8,128)(2,1)} %param.32) | copy-start | bytes 393220
  7.2 592.1 %all-reduce.9.cloned.1.call-start = ((), (), s32[]{:S(2)}) async-start(), calls=%async_computation | async-start | bytes 917504 | tf_op jit(solution)/shard_map/psum | solution.py:281
  12.5 53.5 %collective-permute-start = (bf16[1,8,4096]{2,1,0:T(8,128)(2,1)}, bf16[1,8,4096]{2,1,0:T(8,128)(2,1)}, u32[]{:S(2)}, u32[]{:S(2)}) collective-permute-start(bf16[1,8,4096]{2,1,0:T(8,128)(2,1)} %copy.115), channel_id=1, source_target_pairs={{0,8},{8,16},{16,24},{24,32},{32,40},{40,48},{48,56},{56,64},{64,7... | collective-permute-start | bytes 196616 | tf_op jit(solution)/shard_map/ppermute | solution.py:22
  20.1 45.9 %collective-permute-start.1 = (bf16[1,8,4096]{2,1,0:T(8,128)(2,1)}, bf16[1,8,4096]{2,1,0:T(8,128)(2,1)}, u32[]{:S(2)}, u32[]{:S(2)}) collective-permute-start(bf16[1,8,4096]{2,1,0:T(8,128)(2,1)} %copy.122), channel_id=1, source_target_pairs={{8,0},{16,8},{24,16},{32,24},{40,32},{48,40},{56,48},{64,56},{72,6... | collective-permute-start | bytes 196616 | tf_op jit(solution)/shard_map/ppermute | solution.py:25
  27.4 38.7 %collective-permute-start.2 = (bf16[1,8,4096]{2,1,0:T(8,128)(2,1)}, bf16[1,8,4096]{2,1,0:T(8,128)(2,1)}, u32[]{:S(2)}, u32[]{:S(2)}) collective-permute-start(bf16[1,8,4096]{2,1,0:T(8,128)(2,1)} %copy.129), channel_id=1, source_target_pairs={{0,1},{1,2},{2,3},{3,4},{4,5},{5,6},{6,7},{8,9},{9,10},{10,11},{11... | collective-permute-start | bytes 196616 | tf_op jit(solution)/shard_map/ppermute | solution.py:22
  37.3 28.8 %collective-permute-start.3 = (bf16[1,8,4096]{2,1,0:T(8,128)(2,1)}, bf16[1,8,4096]{2,1,0:T(8,128)(2,1)}, u32[]{:S(2)}, u32[]{:S(2)}) collective-permute-start(bf16[1,8,4096]{2,1,0:T(8,128)(2,1)} %copy.136), channel_id=1, source_target_pairs={{1,0},{2,1},{3,2},{4,3},{5,4},{6,5},{7,6},{9,8},{10,9},{11,10},{12... | collective-permute-start | bytes 196616 | tf_op jit(solution)/shard_map/ppermute | solution.py:25
  77.9 6.0 copy-start.8
  77.9 6.0 copy-start.14
  102.9 11.6 %copy-start.28 = (bf16[64,448]{1,0:T(8,128)(2,1)S(1)}, bf16[64,448]{1,0:T(8,128)(2,1)}, u32[]{:S(2)}) copy-start(bf16[64,448]{1,0:T(8,128)(2,1)} %param.31) | copy-start | bytes 172036
  119.6 11.9 %copy-start.27 = (bf16[1,512,128]{2,1,0:T(8,128)(2,1)S(1)}, bf16[1,512,128]{2,1,0:T(8,128)(2,1)}, u32[]{:S(2)}) copy-start(bf16[1,512,128]{2,1,0:T(8,128)(2,1)} %param.35) | copy-start | bytes 393220
  119.6 11.9 %copy-start.40 = (bf16[128,128]{1,0:T(8,128)(2,1)S(1)}, bf16[128,128]{1,0:T(8,128)(2,1)}, u32[]{:S(2)}) copy-start(bf16[128,128]{1,0:T(8,128)(2,1)} %param.33) | copy-start | bytes 98308
  120.2 1.4 collective-permute-start.4
  121.7 9.0 %collective-permute-start.5 = (bf16[16,8192]{1,0:T(8,128)(2,1)S(1)}, bf16[16,8192]{1,0:T(8,128)(2,1)S(1)}, u32[]{:S(2)}, u32[]{:S(2)}) collective-permute-start(bf16[16,8192]{1,0:T(8,128)(2,1)S(1)} %pad_maximum_fusion), channel_id=1, source_target_pairs={{0,8},{8,0},{16,24},{24,16},{32,40},{40,32},{48,56},{56,48},{64,72... | collective-permute-start | bytes 786440 | tf_op jit(solution)/shard_map/ppermute | solution.py:14
  133.2 9.2 %copy-start.41 = (bf16[128,128]{1,0:T(8,128)(2,1)S(1)}, bf16[128,128]{1,0:T(8,128)(2,1)}, u32[]{:S(2)}) copy-start(bf16[128,128]{1,0:T(8,128)(2,1)} %param.33) | copy-start | bytes 98308
  133.2 7.4 %collective-permute-start.6 = (bf16[16,8192]{1,0:T(8,128)(2,1)S(1)}, bf16[16,8192]{1,0:T(8,128)(2,1)S(1)}, u32[]{:S(2)}, u32[]{:S(2)}) collective-permute-start(bf16[16,8192]{1,0:T(8,128)(2,1)S(1)} %pad_maximum_fusion.1), channel_id=1, source_target_pairs={{0,8},{8,0},{16,24},{24,16},{32,40},{40,32},{48,56},{56,48},{64,72... | collective-permute-start | bytes 786440 | tf_op jit(solution)/shard_map/ppermute | solution.py:14
  140.7 2.7 collective-permute-start.7
  287.6 67.8 %collective-permute-start.9 = (bf16[1,8,4096]{2,1,0:T(8,128)(2,1)}, bf16[1,8,4096]{2,1,0:T(8,128)(2,1)}, u32[]{:S(2)}, u32[]{:S(2)}) collective-permute-start(bf16[1,8,4096]{2,1,0:T(8,128)(2,1)} %fusion.53), channel_id=1, source_target_pairs={{0,8},{8,16},{16,24},{24,32},{32,40},{40,48},{48,56},{56,64},{64,7... | collective-permute-start | bytes 196616 | tf_op jit(solution)/shard_map/ppermute | solution.py:22
  291.3 58.9 %collective-permute-start.10 = (bf16[1,8,4096]{2,1,0:T(8,128)(2,1)}, bf16[1,8,4096]{2,1,0:T(8,128)(2,1)}, u32[]{:S(2)}, u32[]{:S(2)}) collective-permute-start(bf16[1,8,4096]{2,1,0:T(8,128)(2,1)} %fusion.54), channel_id=1, source_target_pairs={{1,0},{2,1},{3,2},{4,3},{5,4},{6,5},{7,6},{9,8},{10,9},{11,10},{12... | collective-permute-start | bytes 196616 | tf_op jit(solution)/shard_map/ppermute | solution.py:25
  293.8 51.4 %collective-permute-start.8 = (bf16[1,8,4096]{2,1,0:T(8,128)(2,1)}, bf16[1,8,4096]{2,1,0:T(8,128)(2,1)}, u32[]{:S(2)}, u32[]{:S(2)}) collective-permute-start(bf16[1,8,4096]{2,1,0:T(8,128)(2,1)} %fusion.52), channel_id=1, source_target_pairs={{8,0},{16,8},{24,16},{32,24},{40,32},{48,40},{56,48},{64,56},{72,6... | collective-permute-start | bytes 196616 | tf_op jit(solution)/shard_map/ppermute | solution.py:25
  295.1 45.2 %collective-permute-start.11 = (bf16[1,8,4096]{2,1,0:T(8,128)(2,1)}, bf16[1,8,4096]{2,1,0:T(8,128)(2,1)}, u32[]{:S(2)}, u32[]{:S(2)}) collective-permute-start(bf16[1,8,4096]{2,1,0:T(8,128)(2,1)} %fusion.55), channel_id=1, source_target_pairs={{0,1},{1,2},{2,3},{3,4},{4,5},{5,6},{6,7},{8,9},{9,10},{10,11},{11... | collective-permute-start | bytes 196616 | tf_op jit(solution)/shard_map/ppermute | solution.py:22
  315.6 6.5 %copy-start.17 = (f32[8,64,1,2,2,1,4,4]{1,7,6,5,4,3,2,0:T(4,128)S(1)}, f32[8,64,1,2,2,1,4,4]{1,7,6,5,4,3,2,0:T(4,128)}, u32[]{:S(2)}) copy-start(f32[8,64,1,2,2,1,4,4]{1,7,6,5,4,3,2,0:T(4,128)} %copy.165) | copy-start | bytes 393220
  315.6 6.7 %copy-start.19 = (f32[8,64,1,2,2,1,4,4]{1,7,6,5,4,3,2,0:T(4,128)S(1)}, f32[8,64,1,2,2,1,4,4]{1,7,6,5,4,3,2,0:T(4,128)}, u32[]{:S(2)}) copy-start(f32[8,64,1,2,2,1,4,4]{1,7,6,5,4,3,2,0:T(4,128)} %copy.169) | copy-start | bytes 393220
  315.7 6.8 %copy-start.16 = (f32[8,64,2,1,2,4,1,4]{1,7,6,5,4,3,2,0:T(4,128)S(1)}, f32[8,64,2,1,2,4,1,4]{1,7,6,5,4,3,2,0:T(4,128)}, u32[]{:S(2)}) copy-start(f32[8,64,2,1,2,4,1,4]{1,7,6,5,4,3,2,0:T(4,128)} %copy.173) | copy-start | bytes 393220
  360.8 243.3 %copy-start.1 = (bf16[128,512]{1,0:T(8,128)(2,1)S(1)}, bf16[128,512]{1,0:T(8,128)(2,1)}, u32[]{:S(2)}) copy-start(bf16[128,512]{1,0:T(8,128)(2,1)} %param.32) | copy-start | bytes 393220
  (33 other events, 79.7 us)
Sparse Core Ops, SparseCore 0:
  340.4 258.8 all-reduce.8
where the time goes:
time: 619 us; the launch traced here: 611 us
  local copies, waits for them, and re-layouts  264 us (43%)
  waiting for transfers between devices  247 us (40%)
  other arithmetic  37.3 us (6%)
  starting transfers between devices  28.8 us (5%)
  matrix products  18.1 us (3%)
  between operations  16.2 us (3%)
    psum x1, waiting for transfers between devices, body(): summed = lax.psum((conv_part, down_part, head_part), ('gx', 'gy'))  235 us
    slice x1, local copies, waits for them, and re-layouts, stack_grad(): moved, plane = minus_back(parts[:, direction + 1], axis_number)  53 us
    convert_element_type x8, local copies, waits for them, and re-layouts, planes(): return rows.astype(jnp.float32).reshape(number, channels, 2, 2, 4, 4)  20 us
    slice x12, local copies, waits for them, and re-layouts, face_of(): lax.index_in_dim(plane, 1 if upper else 0, 2 + axis_number, keepdims=False)  16.3 us
    ppermute x4, starting transfers between devices, padded(): lax.ppermute(lax.slice_in_dim(block, block.shape[dim] - width, None, axis...  15.9 us
    reshape x1, local copies, waits for them, and re-layouts, stack_grad(): parts = taps_grad.reshape(number, 7, channels, 2, 2, 2, 4, 4, 4)  13.2 us
    scatter-add x2, local copies, waits for them, and re-layouts, stack_grad(): grad_cube.at[face_index(direction // 2, direction % 2 == 0)].add(shaped)  12.7 us
  transfers between devices with their start and end apart: 13, of which 5 were waited for; matrix products, arithmetic and copies ran while one was open for 18% of the time, Pallas kernels for 0%

commit v1 on v0

v1 whole, which is shorter than its diff:
```python
import jax
import jax.numpy as jnp
from jax import lax
from jax.experimental import pallas as pl
from jax.experimental.pallas import tpu as pltpu
from jax.sharding import PartitionSpec as P

MESH = pl.DeviceIdType.MESH
F32 = jnp.float32
BF16 = jnp.bfloat16
STRIDE = (16, 4, 1)
GRAD_ROWS = 1024


def ring_z(n_gx):
    return 8 if n_gx % 8 == 0 else n_gx // 2


def dot(a, b, ca, cb):
    return lax.dot_general(a, b, (((ca,), (cb,)), ((), ())), preferred_element_type=F32)


def lanes():
    return lax.broadcasted_iota(jnp.int32, (64, 128), 1)


def flag(value):
    return jnp.broadcast_to(value, (64, 128))


def roll(values, amount):
    amount = amount % 128
    return values if amount == 0 else pltpu.roll(values, amount, 1)


def column(axis, bit, s):
    high, low = s // 2, s % 2
    bits = [high, low]
    bits.insert(axis, bit)
    return bits[0] * 4 + bits[1] * 2 + bits[2]


def field(axis):
    return lax.rem(lax.div(lanes(), STRIDE[axis]), 4)


def pack_face(cols, axis, upper):
    step = STRIDE[axis]
    place = field(axis)
    out = None
    for s in range(4):
        shift = step * (s - 3) if upper else step * s
        moved = roll(cols[column(axis, int(upper), s)], shift)
        out = moved if out is None else jnp.where(place == s, moved, out)
    return out


def shift_minus(cols, axis, face):
    step = STRIDE[axis]
    edge = field(axis) == 0
    out = [None] * 8
    for s in range(4):
        low, high = column(axis, 0, s), column(axis, 1, s)
        out[high] = cols[low]
        out[low] = jnp.where(edge, roll(face, -step * s), roll(cols[high], step))
    return out


def shift_plus(cols, axis, face):
    step = STRIDE[axis]
    edge = field(axis) == 3
    out = [None] * 8
    for s in range(4):
        low, high = column(axis, 0, s), column(axis, 1, s)
        out[low] = cols[high]
        out[high] = jnp.where(edge, roll(face, step * (3 - s)), roll(cols[low], -step))
    return out


def sigmoid(values):
    return 1.0 / (1.0 + jnp.exp(-values))


def silu_grad(values):
    s = sigmoid(values)
    return s * (1.0 + values * (1.0 - s))


def edges(n_gx, n_gy):
    x, y = lax.axis_index("gx"), lax.axis_index("gy")
    return (x == 0, x == n_gx - 1, y == 0, y == n_gy - 1)


def link_of(links, slot, direction, rim):
    value = links[slot, direction]
    if direction < 4:
        return jnp.where(jnp.logical_and(rim[direction], value >= 8), 16, value)
    return value


def selection():
    row = lax.broadcasted_iota(jnp.int32, (512, 512), 0)
    col = lax.broadcasted_iota(jnp.int32, (512, 512), 1)
    return jnp.where(col == lax.rem(row, 64) * 8 + lax.div(row, 64), 1.0, 0.0).astype(BF16)


def pack_kernel(counts, maps, features, down, cube, faces, down_rows, map_out):
    low_half = lanes() < 64
    zero = jnp.zeros((64, 128), BF16)

    def pair(i, carry):
        keep_a = flag(counts[0] - 2 * i) > 0
        keep_b = flag(counts[0] - 2 * i) > 1
        cols = [None] * 8
        for pq in range(4):
            a = jnp.where(keep_a, features[2 * i, :, pq * 128 : pq * 128 + 128], zero)
            b = jnp.where(keep_b, features[2 * i + 1, :, pq * 128 : pq * 128 + 128], zero)
            cols[2 * pq] = jnp.where(low_half, a, roll(b, 64))
            cols[2 * pq + 1] = jnp.where(low_half, roll(a, 64), b)
        for c in range(8):
            cube[i, :, c * 128 : c * 128 + 128] = cols[c]
        for d in range(6):
            faces[d, i] = pack_face(cols, d // 2, d % 2 == 0)
        return carry

    lax.fori_loop(0, 4, pair, 0)
    down_rows[...] = dot(selection(), down[...], 1, 1).astype(BF16)
    lane = lax.broadcasted_iota(jnp.int32, (8, 128), 1)
    table = jnp.zeros((8, 128), jnp.int32)
    for k in range(8):
        table = jnp.where(lane == k, jnp.broadcast_to(maps[0, k], (8, 128)), table)
    map_out[...] = table


def level_kernel(n_gx, n_gy, links, cube, faces, remote, conv, down_rows, taps, hidden, act, octants, pool):
    rim = edges(n_gx, n_gy)
    low_half = lanes() < 64
    zero = jnp.zeros((64, 128), BF16)
    for d in range(6):
        pool[d, 0, 8] = zero
        pool[d, 1, 8] = zero

    def fill(j, carry):
        for d in range(6):
            own = faces[d, j]
            pool[d, 0, j] = own
            pool[d, 1, j] = roll(own, 64)
            far = remote[d, j] if d < 4 else zero
            pool[d, 0, 4 + j] = far
            pool[d, 1, 4 + j] = roll(far, 64) if d < 4 else far
        return carry

    lax.fori_loop(0, 4, fill, 0)

    def pair(i, carry):
        cols = [cube[i, :, c * 128 : c * 128 + 128] for c in range(8)]
        for c in range(8):
            taps[i, 0:64, c * 128 : c * 128 + 128] = cols[c]
        for d in range(6):
            e0 = link_of(links, 2 * i, d, rim)
            e1 = link_of(links, 2 * i + 1, d, rim)
            face = jnp.where(
                low_half,
                pool[d, lax.rem(e0, 2), lax.div(e0, 2)],
                pool[d, 1 - lax.rem(e1, 2), lax.div(e1, 2)],
            )
            moved = (shift_minus if d % 2 == 0 else shift_plus)(cols, d // 2, face)
            for c in range(8):
                taps[i, 64 * (d + 1) : 64 * (d + 2), c * 128 : c * 128 + 128] = moved[c]
        values = dot(conv[...], taps[i], 1, 0)
        hidden[i] = values
        active = (values * sigmoid(values)).astype(BF16)
        for c in range(8):
            act[i, c * 64 : c * 64 + 64, :] = active[:, c * 128 : c * 128 + 128]
        rows = dot(act[i], down_rows[...], 0, 0).astype(BF16)
        octants[2 * i] = rows[:64]
        octants[2 * i + 1] = rows[64:]
        return carry

    lax.fori_loop(0, 4, pair, 0)


def coarse_kernel(maps, own, received, head, grad_in, latent, coarse_grad, head_sum, coarse):
    zero = jnp.zeros((64, 128), BF16)
    for k in range(8):
        e = maps[0, k]
        mine = own[jnp.minimum(e, 7)]
        other = received[jnp.clip(e - 8, 0, 23)]
        row = jnp.where(flag(e) < 8, mine, jnp.where(flag(e) < 32, other, zero))
        coarse[k * 64 : k * 64 + 64, :] = row
    values = coarse[...].astype(F32)
    s = sigmoid(values)
    active = (values * s).astype(BF16)
    latent[0] = dot(active, head[...], 1, 1).astype(BF16)
    grad = grad_in[0]
    back = dot(grad, head[...], 1, 0) * (s * (1.0 + values * (1.0 - s)))
    back = back.astype(BF16)
    for k in range(8):
        coarse_grad[k] = back[k * 64 : k * 64 + 64]
    head_sum[...] = dot(grad, active, 0, 0).astype(BF16)


def backward_kernel(
    n_gx, n_gy, links, maps, far_maps, own, received, hidden, act, taps, down_rows, head_sum,
    grads, hidden_grad, near_faces, far_faces, inverse, pool, conv_acc, down_acc,
):
    rim = edges(n_gx, n_gy)
    lane = lanes()
    zero = jnp.zeros((64, 128), BF16)
    for s in range(8):
        inverse[s] = 32
    for m in range(4):
        for k in range(8):
            e = maps[0, k] if m == 0 else far_maps[m - 1, 0, k]
            slot = lax.rem(e, 8)
            inverse[slot] = jnp.where(lax.div(e, 8) == m, m * 8 + k, inverse[slot])
    for d in range(6):
        for j in range(9):
            pool[d, j] = jnp.zeros((64, 128), F32)
    conv_acc[...] = jnp.zeros_like(conv_acc)
    down_acc[...] = jnp.zeros_like(down_acc)

    def row_of(slot):
        e = inverse[slot]
        mine = own[jnp.minimum(e, 7)]
        other = received[jnp.clip(e - 8, 0, 23)]
        return jnp.where(flag(e) < 8, mine, jnp.where(flag(e) < 32, other, zero))

    def pair(i, carry):
        rows = jnp.concatenate([row_of(2 * i), row_of(2 * i + 1)], axis=0)
        down_acc[...] += dot(act[i], rows, 1, 0)
        patch = dot(down_rows[...], rows, 1, 1)
        cols = []
        for c in range(8):
            slope = silu_grad(hidden[i, :, c * 128 : c * 128 + 128])
            value = (patch[c * 64 : c * 64 + 64] * slope).astype(BF16)
            hidden_grad[i, :, c * 128 : c * 128 + 128] = value
            cols.append(value)
        conv_acc[...] += dot(hidden_grad[i], taps[i], 1, 1)
        for d in range(6):
            face = pack_face(cols, d // 2, d % 2 == 1).astype(F32)
            swapped = roll(face, 64)
            for g in range(2):
                e = link_of(links, 2 * i + g, d, rim)
                half = lax.rem(e, 2)
                row = lax.div(e, 2)
                value = jnp.where(flag(half) == g, face, swapped)
                value = jnp.where(lax.div(lane, 64) == flag(half), value, 0.0)
                pool[d, row] = pool[d, row] + value
        return carry

    lax.fori_loop(0, 4, pair, 0)
    for d in range(6):
        for j in range(4):
            near_faces[d, j] = pool[d, j]
            if d < 4:
                far_faces[d, j] = pool[d, 4 + j].astype(BF16)
    wide = conv_acc[...].astype(BF16)
    for j in range(3):
        grads[j * 64 : j * 64 + 64, :] = wide[:, j * 128 : j * 128 + 128]
    grads[192:256, :] = jnp.concatenate([wide[:, 384:448], jnp.zeros((64, 64), BF16)], axis=1)
    ordered = dot(down_acc[...].astype(BF16), selection(), 0, 0).astype(BF16)
    for j in range(4):
        grads[256 + j * 128 : 384 + j * 128, :] = ordered[:, j * 128 : j * 128 + 128]
    grads[768:896, :] = head_sum[...]
    grads[896:1024, :] = jnp.zeros((128, 128), BF16)


def final_kernel(counts, conv, hidden_grad, near_faces, far_in, out, turned, taps):
    low_half = lanes() < 64
    zero = jnp.zeros((64, 128), F32)
    for d in range(7):
        block = conv[:, d * 64 : d * 64 + 64].astype(F32)
        turned[:, d * 64 : d * 64 + 64] = block.T.astype(BF16)

    def pair(i, carry):
        cols = [hidden_grad[i, :, c * 128 : c * 128 + 128] for c in range(8)]
        for c in range(8):
            taps[0:64, c * 128 : c * 128 + 128] = cols[c]
        for d in range(6):
            face = near_faces[d, i]
            if d < 4:
                face = face + far_in[d, i].astype(F32)
            moved = (shift_plus if d % 2 == 0 else shift_minus)(cols, d // 2, face.astype(BF16))
            for c in range(8):
                taps[64 * (d + 1) : 64 * (d + 2), c * 128 : c * 128 + 128] = moved[c]
        total = dot(turned[...], taps[...], 1, 0)
        keep_a = flag(counts[0] - 2 * i) > 0
        keep_b = flag(counts[0] - 2 * i) > 1
        for pq in range(4):
            even = total[:, pq * 256 : pq * 256 + 128]
            odd = total[:, pq * 256 + 128 : pq * 256 + 256]
            a = jnp.where(low_half, even, roll(odd, 64))
            b = jnp.where(low_half, roll(even, 64), odd)
            out[2 * i, :, pq * 128 : pq * 128 + 128] = jnp.where(keep_a, a, zero).astype(BF16)
            out[2 * i + 1, :, pq * 128 : pq * 128 + 128] = jnp.where(keep_b, b, zero).astype(BF16)
        return carry

    lax.fori_loop(0, 4, pair, 0)


def greet(devices):
    barrier = pltpu.get_barrier_semaphore()
    for device in devices:
        pl.semaphore_signal(barrier, inc=1, device_id=device, device_id_type=MESH)
    pl.semaphore_wait(barrier, len(devices))


def around(n_gx, n_gy):
    x, y = lax.axis_index("gx"), lax.axis_index("gy")
    return (
        (lax.rem(x + 1, n_gx), y),
        (lax.rem(x + n_gx - 1, n_gx), y),
        (x, lax.rem(y + 1, n_gy)),
        (x, lax.rem(y + n_gy - 1, n_gy)),
    )


def partners():
    x, y = lax.axis_index("gx"), lax.axis_index("gy")
    x1 = x + 1 - 2 * lax.rem(x, 2)
    y1 = y + 1 - 2 * lax.rem(y, 2)
    return ((x1, y), (x, y1), (x1, y1))


def run_copies(copies):
    for copy in copies:
        copy.start()
    for copy in copies:
        copy.wait()


def faces_kernel(n_gx, n_gy, faces, table, far, tables, send, recv):
    beside = around(n_gx, n_gy)
    merged = partners()
    greet(beside + (merged[2],))
    copies = []
    for d in range(4):
        copies.append(pltpu.make_async_remote_copy(
            src_ref=faces.at[d], dst_ref=far.at[d], send_sem=send.at[d], recv_sem=recv.at[d],
            device_id=beside[d], device_id_type=MESH,
        ))
    for m in range(3):
        copies.append(pltpu.make_async_remote_copy(
            src_ref=table, dst_ref=tables.at[m], send_sem=send.at[4 + m], recv_sem=recv.at[4 + m],
            device_id=merged[m], device_id_type=MESH,
        ))
    run_copies(copies)


def return_kernel(n_gx, n_gy, faces, far, send, recv):
    beside = around(n_gx, n_gy)
    greet(beside)
    target = (beside[1], beside[0], beside[3], beside[2])
    run_copies([
        pltpu.make_async_remote_copy(
            src_ref=faces.at[d], dst_ref=far.at[d], send_sem=send.at[d], recv_sem=recv.at[d],
            device_id=target[d], device_id_type=MESH,
        )
        for d in range(4)
    ])


def merge_kernel(own, received, send, recv):
    merged = partners()
    greet(merged)
    run_copies([
        pltpu.make_async_remote_copy(
            src_ref=own, dst_ref=received.at[pl.ds(8 * m, 8)], send_sem=send.at[m],
            recv_sem=recv.at[m], device_id=merged[m], device_id_type=MESH,
        )
        for m in range(3)
    ])


def sum_kernel(
    n_gx, n_gy, grads, conv_out, down_out, head_out,
    part_a, sum_a, part_b, sum_b, part_c, part_d, part_e,
    send_a, recv_a, send_b, recv_b, send_c, recv_c, send_d, recv_d, send_e, recv_e,
):
    nz = ring_z(n_gx)
    ny = n_gx // nz
    x, me = lax.axis_index("gx"), lax.axis_index("gy")
    y, z = lax.div(x, nz), lax.rem(x, nz)
    scale = float(2048) ** -0.5
    rows_g = [(x, lax.rem(me + k, n_gy)) for k in range(1, n_gy)]
    rows_z = [(y * nz + lax.rem(z + k, nz), me) for k in range(1, nz)]
    rows_y = [(lax.rem(y + k, ny) * nz + z, me) for k in range(1, ny)]
    greet(rows_g + rows_z + rows_y)

    def send(source, target, sems, k, device):
        return pltpu.make_async_remote_copy(
            src_ref=source, dst_ref=target, send_sem=sems[0].at[k], recv_sem=sems[1].at[k],
            device_id=device, device_id_type=MESH,
        )

    copies = [
        send(grads.at[lax.rem(me + k, n_gy)], part_a.at[k], (send_a, recv_a), k, rows_g[k - 1])
        for k in range(1, n_gy)
    ]
    run_copies(copies)
    total = grads[me].astype(F32)
    for k in range(1, n_gy):
        total = total + part_a[k].astype(F32)
    sum_a[...] = total.astype(BF16)
    copies = [
        send(sum_a.at[lax.rem(z + k, nz)], part_b.at[k], (send_b, recv_b), k, rows_z[k - 1])
        for k in range(1, nz)
    ]
    run_copies(copies)
    total = sum_a[z].astype(F32)
    for k in range(1, nz):
        total = total + part_b[k].astype(F32)
    sum_b[...] = total
    part_c[y] = total
    copies = [
        send(sum_b, part_c.at[y], (send_c, recv_c), k, rows_y[k - 1]) for k in range(1, ny)
    ]
    run_copies(copies)
    total = part_c[0]
    for k in range(1, ny):
        total = total + part_c[k]
    part_d[z] = total.astype(BF16)
    copies = [
        send(part_d.at[z], part_d.at[z], (send_d, recv_d), k, rows_z[k - 1]) for k in range(1, nz)
    ]
    run_copies(copies)
    part_e[me] = part_d[...]
    copies = [
        send(part_d, part_e.at[me], (send_e, recv_e), k, rows_g[k - 1]) for k in range(1, n_gy)
    ]
    run_copies(copies)
    result = part_e[...].reshape(GRAD_ROWS, 128).astype(F32) * scale
    for j in range(3):
        conv_out[:, j * 128 : j * 128 + 128] = result[j * 64 : j * 64 + 64]
    conv_out[:, 384:448] = result[192:256, :64]
    for j in range(4):
        down_out[:, j * 128 : j * 128 + 128] = result[256 + j * 128 : 384 + j * 128]
    head_out[...] = result[768:896]


VM = pl.BlockSpec(memory_space=pltpu.VMEM)
SM = pl.BlockSpec(memory_space=pltpu.SMEM)
ANY = pl.BlockSpec(memory_space=pl.ANY)
DMA = pltpu.SemaphoreType.DMA


def shape(*dims, dtype=BF16):
    return jax.ShapeDtypeStruct(dims, dtype)


def call(kernel, name, ins, outs, shapes, scratch=(), channel=None):
    if channel is None:
        params = pltpu.CompilerParams()
    else:
        params = pltpu.CompilerParams(collective_id=channel, has_side_effects=True)
    return pl.pallas_call(
        kernel, name=name, in_specs=ins, out_specs=outs, out_shape=shapes,
        scratch_shapes=list(scratch), compiler_params=params,
    )


def bind(kernel, *fixed):
    def run(*refs):
        kernel(*fixed, *refs)

    return run


def body(
    features, neighbours, counts, conv_weight, down_weight, head_weight, coarse_map, latent_grad
):
    n_gx, n_gy = lax.axis_size("gx"), lax.axis_size("gy")
    nz = ring_z(n_gx)
    ny = n_gx // nz
    cube, faces, down_rows, table = call(
        pack_kernel, "pack", [SM, SM, VM, VM], [VM] * 4,
        [shape(4, 64, 1024), shape(6, 4, 64, 128), shape(512, 128), shape(8, 128, dtype=jnp.int32)],
    )(counts, coarse_map, features, down_weight)
    remote, tables = call(
        bind(faces_kernel, n_gx, n_gy), "faces", [ANY, ANY], [ANY, ANY],
        [shape(4, 4, 64, 128), shape(3, 8, 128, dtype=jnp.int32)], [DMA((7,)), DMA((7,))], 0,
    )(faces, table)
    taps, hidden, act, octants = call(
        bind(level_kernel, n_gx, n_gy), "level", [SM] + [VM] * 5, [VM] * 4,
        [shape(4, 448, 1024), shape(4, 64, 1024, dtype=F32), shape(4, 512, 128), shape(8, 64, 128)],
        [pltpu.VMEM((6, 2, 9, 64, 128), BF16)],
    )(neighbours, cube, faces, remote, conv_weight, down_rows)
    received = call(
        merge_kernel, "merge_octants", [ANY], ANY, shape(24, 64, 128), [DMA((3,)), DMA((3,))], 1,
    )(octants)
    latent, coarse_grad, head_sum = call(
        coarse_kernel, "coarse", [SM] + [VM] * 4, [VM] * 3,
        [shape(1, 512, 128), shape(8, 64, 128), shape(128, 128)], [pltpu.VMEM((512, 128), BF16)],
    )(coarse_map, octants, received, head_weight, latent_grad)
    grad_received = call(
        merge_kernel, "merge_grads", [ANY], ANY, shape(24, 64, 128), [DMA((3,)), DMA((3,))], 2,
    )(coarse_grad)
    grads, hidden_grad, near_faces, far_faces = call(
        bind(backward_kernel, n_gx, n_gy), "backward", [SM] * 3 + [VM] * 7, [VM] * 4,
        [shape(GRAD_ROWS, 128), shape(4, 64, 1024), shape(6, 4, 64, 128, dtype=F32), shape(4, 4, 64, 128)],
        [
            pltpu.SMEM((8,), jnp.int32), pltpu.VMEM((6, 9, 64, 128), F32),
            pltpu.VMEM((64, 448), F32), pltpu.VMEM((512, 128), F32),
        ],
    )(
        neighbours, coarse_map, tables, coarse_grad, grad_received, hidden, act, taps, down_rows,
        head_sum,
    )
    far_in = call(
        bind(return_kernel, n_gx, n_gy), "return_faces", [ANY], ANY, shape(4, 4, 64, 128),
        [DMA((4,)), DMA((4,))], 3,
    )(far_faces)
    features_grad = call(
        final_kernel, "final", [SM] + [VM] * 4, VM, shape(8, 64, 512),
        [pltpu.VMEM((64, 448), BF16), pltpu.VMEM((448, 1024), BF16)],
    )(counts, conv_weight, hidden_grad, near_faces, far_in)
    per = GRAD_ROWS // (n_gy * nz)
    conv_grad, down_grad, head_grad = call(
        bind(sum_kernel, n_gx, n_gy), "sum_grads", [VM], [VM] * 3,
        [shape(64, 448, dtype=F32), shape(128, 512, dtype=F32), shape(128, 128, dtype=F32)],
        [
            pltpu.VMEM((n_gy, nz, per, 128), BF16), pltpu.VMEM((nz, per, 128), BF16),
            pltpu.VMEM((nz, per, 128), BF16), pltpu.VMEM((per, 128), F32),
            pltpu.VMEM((ny, per, 128), F32), pltpu.VMEM((nz, per, 128), BF16),
            pltpu.VMEM((n_gy, nz, per, 128), BF16),
            DMA((n_gy,)), DMA((n_gy,)), DMA((nz,)), DMA((nz,)), DMA((ny,)), DMA((ny,)),
            DMA((nz,)), DMA((nz,)), DMA((n_gy,)), DMA((n_gy,)),
        ],
        4,
    )(grads.reshape(n_gy, nz, per, 128))
    return (latent, features_grad, conv_grad, down_grad, head_grad)


def solution(mesh):
    placed = (
        P(("gx", "gy"), None, None),
        P(("gx", "gy"), None),
        P(("gx", "gy")),
        P(),
        P(),
        P(),
        P(("gx", "gy"), None),
        P(("gx", "gy"), None, None),
    )
    return jax.shard_map(
        body,
        mesh=mesh,
        in_specs=placed,
        out_specs=(P(("gx", "gy"), None, None), P(("gx", "gy"), None, None), P(), P(), P()),
        check_vma=False,
    )
```

time: 619 us -> 95.9 us (0.15); the launches traced: 611 us -> 95.6 us
  local copies, waits for them, and re-layouts: 264 us -> 4.71 us
  waiting for transfers between devices: 247 us -> 0 us
  Pallas kernels: 0 us -> 89.5 us
  other arithmetic: 37.3 us -> 0 us
  starting transfers between devices: 28.8 us -> 0 us
  matrix products: 18.1 us -> 0 us
  between operations: 16.2 us -> 1.32 us
    psum x1 -> x0, waiting for transfers between devices: 235 us -> none  [body(): summed = lax.psum((conv_part, down_part, head_part), ('gx', 'gy'))]
    slice x57 -> x0, local copies, waits for them, and re-layouts: 121 us -> none  [the longest x1 53 us: stack_grad(): moved, plane = minus_back(parts[:, direction + 1], axis_number)]
    pallas_call x0 -> x10, Pallas kernels: none -> 89.5 us  [the longest x1 28 us: body(): call(bind(sum_kernel, n_gx, n_gy), 'sum_grads', [VM], [VM] * 3, [shape(64...]
    another operation x33 -> x0, local copies, waits for them, and re-layouts: 49.4 us -> none
    ppermute x12 -> x0, starting transfers between devices: 28.8 us -> none  [the longest x4 15.9 us: padded(): lax.ppermute(lax.slice_in_dim(block, block.shape[dim] - width, None, axis...]
    reshape x4 -> x0, local copies, waits for them, and re-layouts: 26.8 us -> none  [the longest x1 13.2 us: stack_grad(): parts = taps_grad.reshape(number, 7, channels, 2, 2, 2, 4, 4, 4)]
    convert_element_type x11 -> x0, local copies, waits for them, and re-layouts: 20.1 us -> none  [the longest x8 20 us: planes(): return rows.astype(jnp.float32).reshape(number, channels, 2, 2, 4, 4)]
    dot_general x9 -> x0, matrix products: 18.1 us -> none  [the longest x1 4.57 us: body(): jnp.einsum('ok,bkv->bov', conv_weight, taps, preferred_element_type=jnp.f...]
  transfers between devices with their start and end apart: 13 -> 0, of which waited for: 5 -> 0; matrix products, arithmetic and copies ran while one was open for 18% -> 0% of each run, Pallas kernels for 0% -> 0%
where the time goes in v1:
time: 95.9 us; the launch traced here: 95.6 us
  Pallas kernels  89.5 us (93%)
  local copies, waits for them, and re-layouts  4.71 us (5%)
  between operations  1.32 us (1%)
    pallas_call x1, Pallas kernels, body(): call(bind(sum_kernel, n_gx, n_gy), 'sum_grads', [VM], [VM] * 3, [shape(64...  28 us
    pallas_call x1, Pallas kernels, body(): call(bind(faces_kernel, n_gx, n_gy), 'faces', [ANY, ANY], [ANY, ANY], [sh...  13.6 us
    pallas_call x1, Pallas kernels, body(): call(merge_kernel, 'merge_octants', [ANY], ANY, shape(24, 64, 128), [DMA(...  9.4 us
    pallas_call x1, Pallas kernels, body(): call(merge_kernel, 'merge_grads', [ANY], ANY, shape(24, 64, 128), [DMA((3...  8.4 us
    pallas_call x1, Pallas kernels, body(): call(bind(return_kernel, n_gx, n_gy), 'return_faces', [ANY], ANY, shape(4...  6.99 us
    pallas_call x1, Pallas kernels, body(): call(bind(level_kernel, n_gx, n_gy), 'level', [SM] + [VM] * 5, [VM] * 4,...  6.87 us
    pallas_call x1, Pallas kernels, body(): call(bind(backward_kernel, n_gx, n_gy), 'backward', [SM] * 3 + [VM] * 7,...  6.34 us
    pallas_call x1, Pallas kernels, body(): call(final_kernel, 'final', [SM] + [VM] * 4, VM, shape(8, 64, 512), [pltp...  4.92 us

profile of v1, /device:TPU:1, one launch (start us, length us, event | category | flops | bytes accessed | tf_op | source)
XLA Modules:
  0.0 95.6 jit_solution(2433811713209199433)
XLA Ops:
  1.3 3.0 %pack.1 = (bf16[4,64,1024]{2,1,0:T(8,128)(2,1)}, bf16[6,4,64,128]{3,2,1,0:T(8,128)(2,1)}, bf16[512,128]{1,0:T(8,128)(2,1)}, s32[8,128]{1,0:T(8,128)}) custom-call(s32[1]{0:T(128)S(6)} %copy.16.counts, s32[1,8]{1,0:T(1,128)} %refs_1_.1, bf16[8,64,512]{2,1,0:T(8,128)(2,1)} %features.1, bf16[128,512]{1,0:T(8,128)(2,1)} %down.1), custom_call_target="tpu_custom_call" | custom-call | tf_op jit(solution)/shard_map/pack/pallas_call | solution.py:476
  4.3 13.6 %faces.1 = (bf16[4,4,64,128]{3,2,1,0:T(8,128)(2,1)}, s32[3,8,128]{2,1,0:T(8,128)}) custom-call(bf16[6,4,64,128]{3,2,1,0:T(8,128)(2,1)} %get-tuple-element.26.refs_0_.refs_2_, s32[8,128]{1,0:T(8,128)} %get-tuple-element.27.refs_1_), custom_call_target="tpu_custom_call" | custom-call | tf_op jit(solution)/shard_map/faces/pallas_call | solution.py:480
  17.9 6.9 %level.1 = (bf16[4,448,1024]{2,1,0:T(8,128)(2,1)}, f32[4,64,1024]{2,1,0:T(8,128)}, bf16[4,512,128]{2,1,0:T(8,128)(2,1)}, bf16[8,64,128]{2,1,0:T(8,128)(2,1)}) custom-call(s32[8,6]{1,0:T(8,128)} %refs_0_.3, bf16[4,64,1024]{2,1,0:T(8,128)(2,1)} %get-tuple-element.25.refs_1_, bf16[6,4,64,128]{3,2,1,0:T(8,128)(2,1)} %get-tuple-element.26.refs_0_.refs_2_, ...), custom_call_target="tpu_custom_call" | custom-call | tf_op jit(solution)/shard_map/level/pallas_call | solution.py:484
  24.7 9.4 %merge_octants.1.received = bf16[24,64,128]{2,1,0:T(8,128)(2,1)} custom-call(bf16[8,64,128]{2,1,0:T(8,128)(2,1)} %get-tuple-element.30.own), custom_call_target="tpu_custom_call" | custom-call | tf_op jit(solution)/shard_map/merge_octants/pallas_call | solution.py:489
  34.1 2.0 %coarse.1 = (bf16[1,512,128]{2,1,0:T(8,128)(2,1)}, bf16[8,64,128]{2,1,0:T(8,128)(2,1)}, bf16[128,128]{1,0:T(8,128)(2,1)}) custom-call(s32[1,8]{1,0:T(1,128)} %refs_1_.1, bf16[8,64,128]{2,1,0:T(8,128)(2,1)} %get-tuple-element.30.own, bf16[24,64,128]{2,1,0:T(8,128)(2,1)} %merge_octants.1.received, bf16[128,128]{1,0:T(8,128)(2,1)} %head.1, ...), custom_call_target="tpu_custom_call" | custom-call | tf_op jit(solution)/shard_map/coarse/pallas_call | solution.py:492
  36.2 8.4 %merge_grads.1.refs_4_ = bf16[24,64,128]{2,1,0:T(8,128)(2,1)} custom-call(bf16[8,64,128]{2,1,0:T(8,128)(2,1)} %get-tuple-element.33.own.refs_3_), custom_call_target="tpu_custom_call" | custom-call | tf_op jit(solution)/shard_map/merge_grads/pallas_call | solution.py:496
  44.6 6.3 %backward.1 = (bf16[1024,128]{1,0:T(8,128)(2,1)}, bf16[4,64,1024]{2,1,0:T(8,128)(2,1)}, f32[6,4,64,128]{3,2,1,0:T(8,128)}, bf16[4,4,64,128]{3,2,1,0:T(8,128)(2,1)}) custom-call(s32[8,6]{1,0:T(8,128)} %refs_0_.3, s32[1,8]{1,0:T(1,128)} %refs_1_.1, s32[3,8,128]{2,1,0:T(8,128)} %get-tuple-element.32.refs_2_, bf16[8,64,128]{2,1,0:T(8,128)(2,1)} %get-tuple-element.33.own.refs_3_, ...), custom_call_target="tpu_custom_call" | custom-call | tf_op jit(solution)/shard_map/backward/pallas_call | solution.py:499
  50.9 7.0 %return_faces.1.far_in = bf16[4,4,64,128]{3,2,1,0:T(8,128)(2,1)} custom-call(bf16[4,4,64,128]{3,2,1,0:T(8,128)(2,1)} %get-tuple-element.40.refs_0_), custom_call_target="tpu_custom_call" | custom-call | tf_op jit(solution)/shard_map/return_faces/pallas_call | solution.py:510
  57.9 4.9 %final.1 = bf16[8,64,512]{2,1,0:T(8,128)(2,1)} custom-call(s32[1]{0:T(128)S(6)} %copy.16.counts, bf16[64,448]{1,0:T(8,128)(2,1)} %conv.1, bf16[4,64,1024]{2,1,0:T(8,128)(2,1)} %get-tuple-element.38.hidden_grad, f32[6,4,64,128]{3,2,1,0:T(8,128)} %get-tuple-element.39.near_faces, bf16[4,4,64,128]{3,2,1,0:T(8,128)(2,1)} %return_faces.1.far_in), custom_call_target="tpu_custom_call" | custom-call | tf_op jit(solution)/shard_map/final/pallas_call | solution.py:514
  62.8 28.0 %sum_grads.1 = (f32[64,448]{1,0:T(8,128)}, f32[128,512]{1,0:T(8,128)}, f32[128,128]{1,0:T(8,128)}) custom-call(bf16[8,8,16,128]{3,2,1,0:T(8,128)(2,1)} %bitcast.1), custom_call_target="tpu_custom_call" | custom-call | tf_op jit(solution)/shard_map/sum_grads/pallas_call | solution.py:519
  90.8 1.6 %copy.17 = f32[64,448]{1,0:T(8,128)} copy(f32[64,448]{1,0:T(8,128)} %get-tuple-element.52) | data formatting | bytes 229376
  92.4 1.7 %copy.18 = f32[128,512]{1,0:T(8,128)} copy(f32[128,512]{1,0:T(8,128)} %get-tuple-element.53) | data formatting | bytes 524288
  94.1 1.5 %copy.19 = f32[128,128]{1,0:T(8,128)} copy(f32[128,128]{1,0:T(8,128)} %get-tuple-element.54) | data formatting | bytes 131072

commit v2 on v1

v2 whole, which is shorter than its diff:
```python
import jax
import jax.numpy as jnp
from jax import lax
from jax.experimental import pallas as pl
from jax.experimental.pallas import tpu as pltpu
from jax.sharding import PartitionSpec as P

MESH = pl.DeviceIdType.MESH
F32 = jnp.float32
BF16 = jnp.bfloat16
STRIDE = (16, 4, 1)
GRAD_ROWS = 1024


def ring_z(n_gx):
    return 8 if n_gx % 8 == 0 else n_gx // 2


def dot(a, b, ca, cb):
    return lax.dot_general(a, b, (((ca,), (cb,)), ((), ())), preferred_element_type=F32)


def lanes():
    return lax.broadcasted_iota(jnp.int32, (64, 128), 1)


def flag(value):
    return jnp.broadcast_to(value, (64, 128))


def roll(values, amount):
    amount = amount % 128
    return values if amount == 0 else pltpu.roll(values, amount, 1)


def column(axis, bit, s):
    high, low = s // 2, s % 2
    bits = [high, low]
    bits.insert(axis, bit)
    return bits[0] * 4 + bits[1] * 2 + bits[2]


def field(axis):
    return lax.rem(lax.div(lanes(), STRIDE[axis]), 4)


def pack_face(cols, axis, upper):
    step = STRIDE[axis]
    place = field(axis)
    out = None
    for s in range(4):
        shift = step * (s - 3) if upper else step * s
        moved = roll(cols[column(axis, int(upper), s)], shift)
        out = moved if out is None else jnp.where(place == s, moved, out)
    return out


def shift_minus(cols, axis, face):
    step = STRIDE[axis]
    edge = field(axis) == 0
    out = [None] * 8
    for s in range(4):
        low, high = column(axis, 0, s), column(axis, 1, s)
        out[high] = cols[low]
        out[low] = jnp.where(edge, roll(face, -step * s), roll(cols[high], step))
    return out


def shift_plus(cols, axis, face):
    step = STRIDE[axis]
    edge = field(axis) == 3
    out = [None] * 8
    for s in range(4):
        low, high = column(axis, 0, s), column(axis, 1, s)
        out[low] = cols[high]
        out[high] = jnp.where(edge, roll(face, step * (3 - s)), roll(cols[low], -step))
    return out


def sigmoid(values):
    return 1.0 / (1.0 + jnp.exp(-values))


def silu_grad(values):
    s = sigmoid(values)
    return s * (1.0 + values * (1.0 - s))


def edges(n_gx, n_gy):
    x, y = lax.axis_index("gx"), lax.axis_index("gy")
    return (x == 0, x == n_gx - 1, y == 0, y == n_gy - 1)


def link_of(links, slot, direction, rim):
    value = links[slot, direction]
    if direction < 4:
        return jnp.where(jnp.logical_and(rim[direction], value >= 8), 16, value)
    return value


def selection():
    row = lax.broadcasted_iota(jnp.int32, (512, 512), 0)
    col = lax.broadcasted_iota(jnp.int32, (512, 512), 1)
    return jnp.where(col == lax.rem(row, 64) * 8 + lax.div(row, 64), 1.0, 0.0).astype(BF16)


def around(n_gx, n_gy):
    x, y = lax.axis_index("gx"), lax.axis_index("gy")
    return (
        (lax.rem(x + 1, n_gx), y),
        (lax.rem(x + n_gx - 1, n_gx), y),
        (x, lax.rem(y + 1, n_gy)),
        (x, lax.rem(y + n_gy - 1, n_gy)),
    )


def partners():
    x, y = lax.axis_index("gx"), lax.axis_index("gy")
    x1 = x + 1 - 2 * lax.rem(x, 2)
    y1 = y + 1 - 2 * lax.rem(y, 2)
    return ((x1, y), (x, y1), (x1, y1))


def step_kernel(
    n_gx, n_gy, counts, links, maps, features, conv, down, head, grad_in,
    latent, out, total,
    faces, far, table, tables, down_rows, turned, pool, taps, hidden, act, octants, received,
    coarse_act, coarse_grad, grad_received, inverse, hidden_grad, planes, near, far_out, far_in,
    conv_acc, down_acc, final_taps, grads, part_a, sum_a, part_b, sum_b, part_c, part_d, part_e,
    face_s, face_r, merge_s, merge_r, back_s, back_r, ret_s, ret_r,
    send_a, recv_a, send_b, recv_b, send_c, recv_c, send_d, recv_d, send_e, recv_e,
):
    nz = ring_z(n_gx)
    ny = n_gx // nz
    x, me = lax.axis_index("gx"), lax.axis_index("gy")
    y, z = lax.div(x, nz), lax.rem(x, nz)
    beside = around(n_gx, n_gy)
    merged = partners()
    rows_g = [(x, lax.rem(me + k, n_gy)) for k in range(1, n_gy)]
    rows_z = [(y * nz + lax.rem(z + k, nz), me) for k in range(1, nz)]
    rows_y = [(lax.rem(y + k, ny) * nz + z, me) for k in range(1, ny)]
    everyone = list(beside) + list(merged) + rows_g + rows_z + rows_y
    rim = edges(n_gx, n_gy)
    low_half = lanes() < 64
    zero = jnp.zeros((64, 128), BF16)

    def send(source, target, sends, recvs, k, device):
        return pltpu.make_async_remote_copy(
            src_ref=source, dst_ref=target, send_sem=sends.at[k], recv_sem=recvs.at[k],
            device_id=device, device_id_type=MESH,
        )

    barrier = pltpu.get_barrier_semaphore()
    for device in everyone:
        pl.semaphore_signal(barrier, inc=1, device_id=device, device_id_type=MESH)

    def pack(i, carry):
        keep_a = flag(counts[0] - 2 * i) > 0
        keep_b = flag(counts[0] - 2 * i) > 1
        cols = [None] * 8
        for pq in range(4):
            a = jnp.where(keep_a, features[2 * i, :, pq * 128 : pq * 128 + 128], zero)
            b = jnp.where(keep_b, features[2 * i + 1, :, pq * 128 : pq * 128 + 128], zero)
            cols[2 * pq] = jnp.where(low_half, a, roll(b, 64))
            cols[2 * pq + 1] = jnp.where(low_half, roll(a, 64), b)
        for d in range(6):
            faces[d, i] = pack_face(cols, d // 2, d % 2 == 0)
        for c in range(8):
            taps[i, 0:64, c * 128 : c * 128 + 128] = cols[c]
        return carry

    lane = lax.broadcasted_iota(jnp.int32, (8, 128), 1)
    values = jnp.full((8, 128), -1, jnp.int32)
    for k in range(8):
        values = jnp.where(lane == k, jnp.broadcast_to(maps[0, k], (8, 128)), values)
    table[...] = values
    lax.fori_loop(0, 4, pack, 0)
    down_rows[...] = dot(selection(), down[...], 1, 1).astype(BF16)
    pl.semaphore_wait(barrier, len(everyone))
    face_copies = [
        send(faces.at[d], far.at[d], face_s, face_r, d, beside[d]) for d in range(4)
    ] + [send(table, tables.at[m], face_s, face_r, 4 + m, merged[m]) for m in range(3)]
    for copy in face_copies:
        copy.start()
    for d in range(6):
        pool[d, 0, 8] = zero
        pool[d, 1, 8] = zero

    def fill(j, carry):
        for d in range(6):
            own = faces[d, j]
            pool[d, 0, j] = own
            pool[d, 1, j] = roll(own, 64)
            if d >= 4:
                pool[d, 0, 4 + j] = zero
                pool[d, 1, 4 + j] = zero
        return carry

    lax.fori_loop(0, 4, fill, 0)

    def tap(i, d):
        cols = [taps[i, 0:64, c * 128 : c * 128 + 128] for c in range(8)]
        e0 = link_of(links, 2 * i, d, rim)
        e1 = link_of(links, 2 * i + 1, d, rim)
        face = jnp.where(
            low_half,
            pool[d, lax.rem(e0, 2), lax.div(e0, 2)],
            pool[d, 1 - lax.rem(e1, 2), lax.div(e1, 2)],
        )
        moved = (shift_minus if d % 2 == 0 else shift_plus)(cols, d // 2, face)
        for c in range(8):
            taps[i, 64 * (d + 1) : 64 * (d + 2), c * 128 : c * 128 + 128] = moved[c]

    def upright(i, carry):
        tap(i, 4)
        tap(i, 5)
        return carry

    lax.fori_loop(0, 4, upright, 0)
    for d in range(7):
        block = conv[:, d * 64 : d * 64 + 64].astype(F32)
        turned[:, d * 64 : d * 64 + 64] = block.T.astype(BF16)
    for copy in face_copies:
        copy.wait()

    def fill_far(j, carry):
        for d in range(4):
            pool[d, 0, 4 + j] = far[d, j]
            pool[d, 1, 4 + j] = roll(far[d, j], 64)
        return carry

    lax.fori_loop(0, 4, fill_far, 0)

    def chunk(source, target, sends, recvs, i, leg):
        rows = (source if leg < 2 else target).at[pl.ds(2 * i, 2)]
        place = target.at[pl.ds(8 * leg + 2 * i, 2)]
        return send(rows, place, sends, recvs, 4 * leg + i, merged[0] if leg == 0 else merged[1])

    def level(i, carry):
        for d in range(4):
            tap(i, d)
        values = dot(conv[...], taps[i], 1, 0)
        hidden[i] = values
        active = (values * sigmoid(values)).astype(BF16)
        for c in range(8):
            act[i, c * 64 : c * 64 + 64, :] = active[:, c * 128 : c * 128 + 128]
        rows = dot(act[i], down_rows[...], 0, 0).astype(BF16)
        octants[2 * i] = rows[:64]
        octants[2 * i + 1] = rows[64:]
        chunk(octants, received, merge_s, merge_r, i, 0).start()
        chunk(octants, received, merge_s, merge_r, i, 1).start()
        return carry

    lax.fori_loop(0, 4, level, 0)

    def relay(source, target, sends, recvs):
        def one(i, carry):
            chunk(source, target, sends, recvs, i, 0).wait_recv()
            chunk(source, target, sends, recvs, i, 2).start()
            return carry

        def rest(i, carry):
            chunk(source, target, sends, recvs, i, 0).wait_send()
            chunk(source, target, sends, recvs, i, 1).wait()
            chunk(source, target, sends, recvs, i, 2).wait()
            return carry

        lax.fori_loop(0, 4, one, 0)
        lax.fori_loop(0, 4, rest, 0)

    relay(octants, received, merge_s, merge_r)

    def merged_row(e, own, other):
        mine = own[jnp.clip(e, 0, 7)]
        theirs = other[jnp.clip(e - 8, 0, 23)]
        return jnp.where(flag(e) < 8, mine, jnp.where(flag(e) < 32, theirs, zero))

    def coarse(c, carry):
        values = jnp.concatenate([
            merged_row(maps[0, 2 * c], octants, received),
            merged_row(maps[0, 2 * c + 1], octants, received),
        ], axis=0).astype(F32)
        s = sigmoid(values)
        coarse_act[c] = (values * s).astype(BF16)
        back = dot(grad_in[c], head[...], 1, 0) * (s * (1.0 + values * (1.0 - s)))
        back = back.astype(BF16)
        coarse_grad[2 * c] = back[:64]
        coarse_grad[2 * c + 1] = back[64:]
        chunk(coarse_grad, grad_received, back_s, back_r, c, 0).start()
        chunk(coarse_grad, grad_received, back_s, back_r, c, 1).start()
        return carry

    lax.fori_loop(0, 4, coarse, 0)
    active = coarse_act[...].reshape(512, 128)
    latent[...] = dot(active, head[...], 1, 1).astype(BF16)
    grads[6] = dot(grad_in[...].reshape(512, 128), active, 0, 0).astype(BF16)
    grads[7] = jnp.zeros((128, 128), BF16)
    for s in range(8):
        found = jnp.zeros((8, 128), jnp.int32)
        for m in range(4):
            entries = table[...] if m == 0 else tables[m - 1]
            found = jnp.where(entries == m * 8 + s, m * 8 + lane - 32, found)
        inverse[s] = jnp.clip(jnp.sum(found[0:1, :]) + 32, 0, 32)
    conv_acc[...] = jnp.zeros_like(conv_acc)
    down_acc[...] = jnp.zeros_like(down_acc)
    relay(coarse_grad, grad_received, back_s, back_r)

    def backward(i, carry):
        rows = jnp.concatenate([
            merged_row(inverse[2 * i], coarse_grad, grad_received),
            merged_row(inverse[2 * i + 1], coarse_grad, grad_received),
        ], axis=0)
        down_acc[...] += dot(act[i], rows, 1, 0)
        patch = dot(down_rows[...], rows, 1, 1)
        for c in range(8):
            slope = silu_grad(hidden[i, :, c * 128 : c * 128 + 128])
            value = (patch[c * 64 : c * 64 + 64] * slope).astype(BF16)
            hidden_grad[i, :, c * 128 : c * 128 + 128] = value
        conv_acc[...] += dot(hidden_grad[i], taps[i], 1, 1)
        return carry

    lax.fori_loop(0, 4, backward, 0)
    wide = conv_acc[...].astype(BF16)
    grads[0, 0:64, :] = wide[:, 0:128]
    grads[0, 64:128, :] = wide[:, 128:256]
    grads[1, 0:64, :] = wide[:, 256:384]
    grads[1, 64:128, :] = jnp.concatenate([wide[:, 384:448], jnp.zeros((64, 64), BF16)], axis=1)
    ordered = dot(down_acc[...].astype(BF16), selection(), 0, 0).astype(BF16)
    for j in range(4):
        grads[2 + j] = ordered[:, j * 128 : j * 128 + 128]
    copies_a = [
        send(grads.at[lax.rem(me + k, n_gy)], part_a.at[k], send_a, recv_a, k, rows_g[k - 1])
        for k in range(1, n_gy)
    ]
    for copy in copies_a:
        copy.start()

    def plane(i, carry):
        cols = [hidden_grad[i, :, c * 128 : c * 128 + 128] for c in range(8)]
        for d in range(6):
            face = pack_face(cols, d // 2, d % 2 == 1)
            planes[d, 0, i] = face.astype(F32)
            planes[d, 1, i] = roll(face, 64).astype(F32)
        return carry

    lax.fori_loop(0, 4, plane, 0)

    def gathered(d, j):
        out = jnp.zeros((64, 128), F32)
        for i in range(4):
            e0 = link_of(links, 2 * i, d, rim)
            e1 = link_of(links, 2 * i + 1, d, rim)
            straight = jnp.where(low_half, flag(e0), flag(e1 - 1))
            crossed = jnp.where(low_half, flag(e1), flag(e0 - 1))
            out = out + jnp.where(straight == 2 * j, planes[d, 0, i], 0.0)
            out = out + jnp.where(crossed == 2 * j, planes[d, 1, i], 0.0)
        return out

    def collect_far(j, carry):
        for d in range(4):
            far_out[d, j] = gathered(d, 4 + j).astype(BF16)
        return carry

    def collect_near(j, carry):
        for d in range(6):
            near[d, j] = gathered(d, j)
        return carry

    lax.fori_loop(0, 4, collect_far, 0)
    target = (beside[1], beside[0], beside[3], beside[2])
    returns = [send(far_out.at[d], far_in.at[d], ret_s, ret_r, d, target[d]) for d in range(4)]
    for copy in returns:
        copy.start()
    for copy in copies_a:
        copy.wait()
    result = grads[me].astype(F32)
    for k in range(1, n_gy):
        result = result + part_a[k].astype(F32)
    per = result.shape[0] // nz
    result = result.reshape(nz, per, 128)
    sum_a[...] = result.astype(BF16)
    copies_b = [
        send(sum_a.at[lax.rem(z + k, nz)], part_b.at[k], send_b, recv_b, k, rows_z[k - 1])
        for k in range(1, nz)
    ]
    for copy in copies_b:
        copy.start()
    lax.fori_loop(0, 4, collect_near, 0)
    for copy in copies_b:
        copy.wait()
    result = sum_a[z].astype(F32)
    for k in range(1, nz):
        result = result + part_b[k].astype(F32)
    sum_b[...] = result
    part_c[y] = result
    copies_c = [
        send(sum_b, part_c.at[y], send_c, recv_c, k, rows_y[k - 1]) for k in range(1, ny)
    ]
    for copy in copies_c:
        copy.start()
    for copy in returns:
        copy.wait()

    def final(i, carry):
        cols = [hidden_grad[i, :, c * 128 : c * 128 + 128] for c in range(8)]
        for c in range(8):
            final_taps[0:64, c * 128 : c * 128 + 128] = cols[c]
        for d in range(6):
            face = near[d, i]
            if d < 4:
                face = face + far_in[d, i].astype(F32)
            moved = (shift_plus if d % 2 == 0 else shift_minus)(cols, d // 2, face.astype(BF16))
            for c in range(8):
                final_taps[64 * (d + 1) : 64 * (d + 2), c * 128 : c * 128 + 128] = moved[c]
        values = dot(turned[...], final_taps[...], 1, 0)
        keep_a = flag(counts[0] - 2 * i) > 0
        keep_b = flag(counts[0] - 2 * i) > 1
        for pq in range(4):
            even = values[:, pq * 256 : pq * 256 + 128]
            odd = values[:, pq * 256 + 128 : pq * 256 + 256]
            a = jnp.where(low_half, even, roll(odd, 64))
            b = jnp.where(low_half, roll(even, 64), odd)
            out[2 * i, :, pq * 128 : pq * 128 + 128] = jnp.where(keep_a, a, 0.0).astype(BF16)
            out[2 * i + 1, :, pq * 128 : pq * 128 + 128] = jnp.where(keep_b, b, 0.0).astype(BF16)
        return carry

    lax.fori_loop(0, 2, final, 0)
    for copy in copies_c:
        copy.wait()
    result = part_c[0]
    for k in range(1, ny):
        result = result + part_c[k]
    part_d[z] = result.astype(BF16)
    copies_d = [
        send(part_d.at[z], part_d.at[z], send_d, recv_d, k, rows_z[k - 1]) for k in range(1, nz)
    ]
    for copy in copies_d:
        copy.start()
    lax.fori_loop(2, 4, final, 0)
    for copy in copies_d:
        copy.wait()
    part_e[me] = part_d[...]
    copies_e = [
        send(part_d, part_e.at[me], send_e, recv_e, k, rows_g[k - 1]) for k in range(1, n_gy)
    ]
    for copy in copies_e:
        copy.start()
    for copy in copies_e:
        copy.wait()
    total[...] = part_e[...].reshape(n_gy, nz * per, 128)


def unpack_kernel(latent, features, total, latent_out, features_out, conv_out, down_out, head_out):
    scale = float(2048) ** -0.5
    latent_out[0] = latent[...]
    features_out[...] = features[...]
    rows = total[...].reshape(GRAD_ROWS, 128).astype(F32) * scale
    for j in range(3):
        conv_out[:, j * 128 : j * 128 + 128] = rows[j * 64 : j * 64 + 64]
    conv_out[:, 384:448] = rows[192:256, :64]
    for j in range(4):
        down_out[:, j * 128 : j * 128 + 128] = rows[256 + j * 128 : 384 + j * 128]
    head_out[...] = rows[768:896]


VM = pl.BlockSpec(memory_space=pltpu.VMEM)
SM = pl.BlockSpec(memory_space=pltpu.SMEM)
DMA = pltpu.SemaphoreType.DMA
VMEM = pltpu.VMEM


def shape(*dims, dtype=BF16):
    return jax.ShapeDtypeStruct(dims, dtype)


def bind(kernel, *fixed):
    def run(*refs):
        kernel(*fixed, *refs)

    return run


def body(
    features, neighbours, counts, conv_weight, down_weight, head_weight, coarse_map, latent_grad
):
    n_gx, n_gy = lax.axis_size("gx"), lax.axis_size("gy")
    nz = ring_z(n_gx)
    ny = n_gx // nz
    part = GRAD_ROWS // n_gy
    per = part // nz
    latent, grad, total = pl.pallas_call(
        bind(step_kernel, n_gx, n_gy), name="step", in_specs=[SM] * 3 + [VM] * 5,
        out_specs=[VM] * 3,
        out_shape=[shape(512, 128), shape(8, 64, 512), shape(n_gy, part, 128)],
        scratch_shapes=[
            VMEM((6, 4, 64, 128), BF16), VMEM((4, 4, 64, 128), BF16),
            VMEM((8, 128), jnp.int32), VMEM((3, 8, 128), jnp.int32),
            VMEM((512, 128), BF16), VMEM((64, 448), BF16), VMEM((6, 2, 9, 64, 128), BF16),
            VMEM((4, 448, 1024), BF16), VMEM((4, 64, 1024), F32), VMEM((4, 512, 128), BF16),
            VMEM((8, 64, 128), BF16), VMEM((24, 64, 128), BF16),
            VMEM((4, 128, 128), BF16), VMEM((8, 64, 128), BF16), VMEM((24, 64, 128), BF16),
            pltpu.SMEM((8,), jnp.int32), VMEM((4, 64, 1024), BF16), VMEM((6, 2, 4, 64, 128), F32),
            VMEM((6, 4, 64, 128), F32), VMEM((4, 4, 64, 128), BF16), VMEM((4, 4, 64, 128), BF16),
            VMEM((64, 448), F32), VMEM((512, 128), F32), VMEM((448, 1024), BF16),
            VMEM((n_gy, part, 128), BF16), VMEM((n_gy, part, 128), BF16),
            VMEM((nz, per, 128), BF16), VMEM((nz, per, 128), BF16), VMEM((per, 128), F32),
            VMEM((ny, per, 128), F32), VMEM((nz, per, 128), BF16),
            VMEM((n_gy, nz, per, 128), BF16),
            DMA((7,)), DMA((7,)), DMA((12,)), DMA((12,)), DMA((12,)), DMA((12,)),
            DMA((4,)), DMA((4,)),
            DMA((n_gy,)), DMA((n_gy,)), DMA((nz,)), DMA((nz,)), DMA((ny,)), DMA((ny,)),
            DMA((nz,)), DMA((nz,)), DMA((n_gy,)), DMA((n_gy,)),
        ],
        compiler_params=pltpu.CompilerParams(collective_id=0, has_side_effects=True),
    )(
        counts, neighbours, coarse_map, features, conv_weight, down_weight, head_weight,
        latent_grad.reshape(4, 128, 128),
    )
    return pl.pallas_call(
        unpack_kernel, name="unpack", in_specs=[VM] * 3, out_specs=[VM] * 5,
        out_shape=[
            shape(1, 512, 128), shape(8, 64, 512), shape(64, 448, dtype=F32),
            shape(128, 512, dtype=F32), shape(128, 128, dtype=F32),
        ],
    )(latent, grad, total)


def solution(mesh):
    placed = (
        P(("gx", "gy"), None, None),
        P(("gx", "gy"), None),
        P(("gx", "gy")),
        P(),
        P(),
        P(),
        P(("gx", "gy"), None),
        P(("gx", "gy"), None, None),
    )
    return jax.shard_map(
        body,
        mesh=mesh,
        in_specs=placed,
        out_specs=(P(("gx", "gy"), None, None), P(("gx", "gy"), None, None), P(), P(), P()),
        check_vma=False,
    )
```

time: 95.9 us -> 59.5 us (0.62)
  Pallas kernels: 89.5 us -> 58 us
  local copies, waits for them, and re-layouts: 4.71 us -> 0 us
    pallas_call x10 -> x2, Pallas kernels: 89.5 us -> 58 us  [the longest x1 55.9 us: body(): pl.pallas_call(bind(step_kernel, n_gx, n_gy), name='step', in_specs=[SM]...]
    unnamed x3 -> x0, local copies, waits for them, and re-layouts: 4.71 us -> none
where the time goes in v2:
time: 59.5 us; the launch traced here: 59.3 us
  Pallas kernels  58 us (97%)
  between operations  1.29 us (2%)
    pallas_call x1, Pallas kernels, body(): pl.pallas_call(bind(step_kernel, n_gx, n_gy), name='step', in_specs=[SM]...  55.9 us
    pallas_call x1, Pallas kernels, body(): pl.pallas_call(unpack_kernel, name='unpack', in_specs=[VM] * 3, out_specs...  2.16 us

profile of v2, /device:TPU:1, one launch (start us, length us, event | category | flops | bytes accessed | tf_op | source)
XLA Modules:
  0.0 59.3 jit_solution(17057660388457674898)
XLA Ops:
  1.3 55.9 %step.1 = (bf16[512,128]{1,0:T(8,128)(2,1)}, bf16[8,64,512]{2,1,0:T(8,128)(2,1)}, bf16[8,128,128]{2,1,0:T(8,128)(2,1)}) custom-call(s32[1]{0:T(128)S(6)} %copy.13.refs_0_, s32[8,6]{1,0:T(8,128)} %refs_1_.1, s32[1,8]{1,0:T(1,128)} %refs_2_.1, bf16[8,64,512]{2,1,0:T(8,128)(2,1)} %refs_3_.1, bf16[64,448]{1,0:T(8,128)(2,1)} %refs_4_.1, ...), custom_call_target="tpu_custom_call" | custom-call | tf_op jit(solution)/shard_map/step/pallas_call | solution.py:491
  57.2 2.2 %unpack.1 = (bf16[1,512,128]{2,1,0:T(8,128)(2,1)}, bf16[8,64,512]{2,1,0:T(8,128)(2,1)}, f32[64,448]{1,0:T(8,128)}, f32[128,512]{1,0:T(8,128)}, f32[128,128]{1,0:T(8,128)}) custom-call(bf16[512,128]{1,0:T(8,128)(2,1)} %get-tuple-element.8.latent, bf16[8,64,512]{2,1,0:T(8,128)(2,1)} %get-tuple-element.9.features, bf16[8,128,128]{2,1,0:T(8,128)(2,1)} %get-tuple-element.10.total), custom_call_target="tpu_custom_call" | custom-call | tf_op jit(solution)/shard_map/unpack/pallas_call | solution.py:519

commit v3 on v2

v3 whole, which is shorter than its diff:
```python
import jax
import jax.numpy as jnp
from jax import lax
from jax.experimental import pallas as pl
from jax.experimental.pallas import tpu as pltpu
from jax.sharding import PartitionSpec as P

MESH = pl.DeviceIdType.MESH
F32 = jnp.float32
BF16 = jnp.bfloat16
STRIDE = (16, 4, 1)
GRAD_ROWS = 1024


def ring_z(n_gx):
    return 8 if n_gx % 8 == 0 else n_gx // 2


def dot(a, b, ca, cb):
    return lax.dot_general(a, b, (((ca,), (cb,)), ((), ())), preferred_element_type=F32)


def lanes():
    return lax.broadcasted_iota(jnp.int32, (64, 128), 1)


def flag(value):
    return jnp.broadcast_to(value, (64, 128))


def roll(values, amount):
    amount = amount % 128
    return values if amount == 0 else pltpu.roll(values, amount, 1)


def column(axis, bit, s):
    high, low = s // 2, s % 2
    bits = [high, low]
    bits.insert(axis, bit)
    return bits[0] * 4 + bits[1] * 2 + bits[2]


def field(axis):
    return lax.rem(lax.div(lanes(), STRIDE[axis]), 4)


def pack_face(cols, axis, upper):
    step = STRIDE[axis]
    place = field(axis)
    out = None
    for s in range(4):
        shift = step * (s - 3) if upper else step * s
        moved = roll(cols[column(axis, int(upper), s)], shift)
        out = moved if out is None else jnp.where(place == s, moved, out)
    return out


def shift_minus(cols, axis, face):
    step = STRIDE[axis]
    edge = field(axis) == 0
    out = [None] * 8
    for s in range(4):
        low, high = column(axis, 0, s), column(axis, 1, s)
        out[high] = cols[low]
        out[low] = jnp.where(edge, roll(face, -step * s), roll(cols[high], step))
    return out


def shift_plus(cols, axis, face):
    step = STRIDE[axis]
    edge = field(axis) == 3
    out = [None] * 8
    for s in range(4):
        low, high = column(axis, 0, s), column(axis, 1, s)
        out[low] = cols[high]
        out[high] = jnp.where(edge, roll(face, step * (3 - s)), roll(cols[low], -step))
    return out


def sigmoid(values):
    return 1.0 / (1.0 + jnp.exp(-values))


def silu_grad(values):
    s = sigmoid(values)
    return s * (1.0 + values * (1.0 - s))


def edges(n_gx, n_gy):
    x, y = lax.axis_index("gx"), lax.axis_index("gy")
    return (x == 0, x == n_gx - 1, y == 0, y == n_gy - 1)


def link_of(links, slot, direction, rim):
    value = links[slot, direction]
    if direction < 4:
        return jnp.where(jnp.logical_and(rim[direction], value >= 8), 16, value)
    return value


def selection():
    row = lax.broadcasted_iota(jnp.int32, (512, 512), 0)
    col = lax.broadcasted_iota(jnp.int32, (512, 512), 1)
    return jnp.where(col == lax.rem(row, 64) * 8 + lax.div(row, 64), 1.0, 0.0).astype(BF16)


def around(n_gx, n_gy):
    x, y = lax.axis_index("gx"), lax.axis_index("gy")
    return (
        (lax.rem(x + 1, n_gx), y),
        (lax.rem(x + n_gx - 1, n_gx), y),
        (x, lax.rem(y + 1, n_gy)),
        (x, lax.rem(y + n_gy - 1, n_gy)),
    )


def partners():
    x, y = lax.axis_index("gx"), lax.axis_index("gy")
    x1 = x + 1 - 2 * lax.rem(x, 2)
    y1 = y + 1 - 2 * lax.rem(y, 2)
    return ((x1, y), (x, y1), (x1, y1))


def step_kernel(
    n_gx, n_gy, counts, links, maps, conv, down, head, features, grad_in,
    latent, out, total,
    blocks, grad_own, grad_far, faces, far, table, tables, down_rows, turned, pool, taps, hidden,
    act, octants, received, inverse, hidden_grad, planes, near, far_out, far_in, conv_acc, down_acc,
    head_acc, final_taps, coarse, latent_own, out_own,
    grads, part_0, sum_0, part_1, part_2, part_3,
    load_s, store_s, face_s, face_r, merge_s, merge_r, back_s, back_r, ret_s, ret_r,
    send_0, recv_0, send_1, recv_1, send_2, recv_2, send_3, recv_3, send_4, recv_4,
):
    nz = ring_z(n_gx)
    ny, nc = n_gx // nz, n_gy // 2
    plane_size = nc * ny
    x, me = lax.axis_index("gx"), lax.axis_index("gy")
    y, z = lax.div(x, nz), lax.rem(x, nz)
    chip, core = lax.div(me, 2), lax.rem(me, 2)
    spot = chip * ny + y
    beside = around(n_gx, n_gy)
    merged = partners()
    mate = merged[1]
    rows_z = [(y * nz + lax.rem(z + k, nz), me) for k in range(1, nz)]
    rows_p, spots = [None], [None]
    for k in range(1, plane_size):
        other_c = lax.rem(chip + k // ny, nc)
        other_y = lax.rem(y + k % ny, ny)
        rows_p.append((other_y * nz + z, other_c * 2 + core))
        spots.append(other_c * ny + other_y)
    everyone = list(beside) + list(merged) + rows_z + rows_p[1:]
    rim = edges(n_gx, n_gy)
    low_half = lanes() < 64
    zero = jnp.zeros((64, 128), BF16)

    def send(source, target, sends, recvs, k, device):
        return pltpu.make_async_remote_copy(
            src_ref=source, dst_ref=target, send_sem=sends.at[k], recv_sem=recvs.at[k],
            device_id=device, device_id_type=MESH,
        )

    barrier = pltpu.get_barrier_semaphore()
    for device in everyone:
        pl.semaphore_signal(barrier, inc=1, device_id=device, device_id_type=MESH)

    def load(i):
        return pltpu.make_async_copy(
            features.at[pl.ds(2 * i, 2)], blocks.at[pl.ds(2 * i, 2)], load_s.at[i]
        )

    for i in range(4):
        load(i).start()
    grad_load = pltpu.make_async_copy(grad_in, grad_own, load_s.at[4])
    grad_load.start()
    lane = lax.broadcasted_iota(jnp.int32, (8, 128), 1)
    values = jnp.full((8, 128), -1, jnp.int32)
    for k in range(8):
        values = jnp.where(lane == k, jnp.broadcast_to(maps[0, k], (8, 128)), values)
    table[...] = values
    down_rows[...] = dot(selection(), down[...], 1, 1).astype(BF16)

    def pack(i, carry):
        load(i).wait()
        keep_a = flag(counts[0] - 2 * i) > 0
        keep_b = flag(counts[0] - 2 * i) > 1
        cols = [None] * 8
        for pq in range(4):
            a = jnp.where(keep_a, blocks[2 * i, :, pq * 128 : pq * 128 + 128], zero)
            b = jnp.where(keep_b, blocks[2 * i + 1, :, pq * 128 : pq * 128 + 128], zero)
            cols[2 * pq] = jnp.where(low_half, a, roll(b, 64))
            cols[2 * pq + 1] = jnp.where(low_half, roll(a, 64), b)
        for d in range(6):
            faces[d, i] = pack_face(cols, d // 2, d % 2 == 0)
        for c in range(8):
            taps[i, 0:64, c * 128 : c * 128 + 128] = cols[c]
        return carry

    lax.fori_loop(0, 4, pack, 0)
    grad_load.wait()
    pl.semaphore_wait(barrier, len(everyone))
    face_copies = [
        send(faces.at[d], far.at[d], face_s, face_r, d, beside[d]) for d in range(4)
    ] + [send(table, tables.at[m], face_s, face_r, 4 + m, merged[m]) for m in range(3)]
    for copy in face_copies:
        copy.start()

    def chunk(source, target, sends, recvs, i, leg):
        rows = (source if leg < 2 else target).at[pl.ds(2 * i, 2)]
        place = target.at[pl.ds(8 * leg + 2 * i, 2)]
        return send(rows, place, sends, recvs, 4 * leg + i, merged[0] if leg == 0 else mate)

    def grad_chunk(i, leg):
        return chunk(grad_own, grad_far, back_s, back_r, i, leg)

    def octant_chunk(i, leg):
        return chunk(octants, received, merge_s, merge_r, i, leg)

    for i in range(4):
        grad_chunk(i, 0).start()
        grad_chunk(i, 1).start()
    for d in range(6):
        pool[d, 0, 8] = zero
        pool[d, 1, 8] = zero

    def fill(j, carry):
        for d in range(6):
            own = faces[d, j]
            pool[d, 0, j] = own
            pool[d, 1, j] = roll(own, 64)
            if d >= 4:
                pool[d, 0, 4 + j] = zero
                pool[d, 1, 4 + j] = zero
        return carry

    lax.fori_loop(0, 4, fill, 0)

    def tap(i, d):
        cols = [taps[i, 0:64, c * 128 : c * 128 + 128] for c in range(8)]
        e0 = link_of(links, 2 * i, d, rim)
        e1 = link_of(links, 2 * i + 1, d, rim)
        face = jnp.where(
            low_half,
            pool[d, lax.rem(e0, 2), lax.div(e0, 2)],
            pool[d, 1 - lax.rem(e1, 2), lax.div(e1, 2)],
        )
        moved = (shift_minus if d % 2 == 0 else shift_plus)(cols, d // 2, face)
        for c in range(8):
            taps[i, 64 * (d + 1) : 64 * (d + 2), c * 128 : c * 128 + 128] = moved[c]

    def upright(i, carry):
        tap(i, 4)
        tap(i, 5)
        return carry

    lax.fori_loop(0, 4, upright, 0)
    for d in range(7):
        block = conv[:, d * 64 : d * 64 + 64].astype(F32)
        turned[:, d * 64 : d * 64 + 64] = block.T.astype(BF16)
    conv_acc[...] = jnp.zeros_like(conv_acc)
    down_acc[...] = jnp.zeros_like(down_acc)
    head_acc[...] = jnp.zeros_like(head_acc)
    for copy in face_copies:
        copy.wait()

    def fill_far(j, carry):
        for d in range(4):
            pool[d, 0, 4 + j] = far[d, j]
            pool[d, 1, 4 + j] = roll(far[d, j], 64)
        return carry

    lax.fori_loop(0, 4, fill_far, 0)

    def level(i, carry):
        for d in range(4):
            tap(i, d)
        values = dot(conv[...], taps[i], 1, 0)
        hidden[i] = values
        active = (values * sigmoid(values)).astype(BF16)
        for c in range(8):
            act[i, c * 64 : c * 64 + 64, :] = active[:, c * 128 : c * 128 + 128]
        rows = dot(act[i], down_rows[...], 0, 0).astype(BF16)
        octants[2 * i] = rows[:64]
        octants[2 * i + 1] = rows[64:]
        octant_chunk(i, 0).start()
        octant_chunk(i, 1).start()
        grad_chunk(i, 0).wait_recv()
        grad_chunk(i, 2).start()
        return carry

    lax.fori_loop(0, 4, level, 0)
    for s in range(8):
        found = jnp.zeros((8, 128), jnp.int32)
        for m in range(4):
            entries = table[...] if m == 0 else tables[m - 1]
            found = jnp.where(entries == m * 8 + s, m * 8 + lane - 32, found)
        inverse[s] = jnp.clip(jnp.sum(found[0:1, :]) + 32, 0, 32)

    def settle(part):
        def rest(i, carry):
            part(i, 0).wait_send()
            part(i, 1).wait()
            part(i, 2).wait()
            return carry

        lax.fori_loop(0, 4, rest, 0)

    settle(grad_chunk)

    def merged_row(e, own, other):
        mine = own[jnp.clip(e, 0, 7)]
        theirs = other[jnp.clip(e - 8, 0, 23)]
        return jnp.where(flag(e) < 8, mine, jnp.where(flag(e) < 32, theirs, zero))

    def backward(i, carry):
        named = jnp.concatenate([
            merged_row(inverse[2 * i], grad_own, grad_far),
            merged_row(inverse[2 * i + 1], grad_own, grad_far),
        ], axis=0)
        values = jnp.concatenate([octants[2 * i], octants[2 * i + 1]], axis=0).astype(F32)
        s = sigmoid(values)
        active = (values * s).astype(BF16)
        head_acc[...] += dot(named, active, 0, 0)
        rows = dot(named, head[...], 1, 0) * (s * (1.0 + values * (1.0 - s)))
        rows = rows.astype(BF16)
        down_acc[...] += dot(act[i], rows, 1, 0)
        patch = dot(down_rows[...], rows, 1, 1)
        for c in range(8):
            slope = silu_grad(hidden[i, :, c * 128 : c * 128 + 128])
            value = (patch[c * 64 : c * 64 + 64] * slope).astype(BF16)
            hidden_grad[i, :, c * 128 : c * 128 + 128] = value
        conv_acc[...] += dot(hidden_grad[i], taps[i], 1, 1)
        return carry

    lax.fori_loop(0, 4, backward, 0)
    wide = conv_acc[...].astype(BF16)
    for j in range(3):
        grads[0, j * 64 : j * 64 + 64, :] = wide[:, j * 128 : j * 128 + 128]
    grads[0, 192:256, :] = jnp.concatenate([wide[:, 384:448], jnp.zeros((64, 64), BF16)], axis=1)
    ordered = dot(down_acc[...].astype(BF16), selection(), 0, 0).astype(BF16)
    for j in range(4):
        row = 256 + 128 * (j % 2) if j < 2 else 128 * (j % 2)
        grads[j // 2, row : row + 128, :] = ordered[:, j * 128 : j * 128 + 128]
    grads[1, 256:384, :] = head_acc[...].astype(BF16)
    grads[1, 384:512, :] = jnp.zeros((128, 128), BF16)
    copy_0 = send(grads.at[1 - core], part_0, send_0, recv_0, 0, mate)
    copy_0.start()

    def relay(i, carry):
        octant_chunk(i, 0).wait_recv()
        octant_chunk(i, 2).start()
        return carry

    lax.fori_loop(0, 4, relay, 0)

    def plane(i, carry):
        cols = [hidden_grad[i, :, c * 128 : c * 128 + 128] for c in range(8)]
        for d in range(6):
            face = pack_face(cols, d // 2, d % 2 == 1)
            planes[d, 0, i] = face.astype(F32)
            planes[d, 1, i] = roll(face, 64).astype(F32)
        return carry

    def gathered(d, j):
        out = jnp.zeros((64, 128), F32)
        for i in range(4):
            e0 = link_of(links, 2 * i, d, rim)
            e1 = link_of(links, 2 * i + 1, d, rim)
            straight = jnp.where(low_half, flag(e0), flag(e1 - 1))
            crossed = jnp.where(low_half, flag(e1), flag(e0 - 1))
            out = out + jnp.where(straight == 2 * j, planes[d, 0, i], 0.0)
            out = out + jnp.where(crossed == 2 * j, planes[d, 1, i], 0.0)
        return out

    def collect_far(j, carry):
        for d in range(4):
            far_out[d, j] = gathered(d, 4 + j).astype(BF16)
        return carry

    def collect_near(j, carry):
        for d in range(6):
            near[d, j] = gathered(d, j)
        return carry

    copy_0.wait()
    result = grads[core].astype(F32) + part_0[...].astype(F32)
    per = result.shape[0] // plane_size
    sum_0[...] = result.astype(BF16).reshape(plane_size, per, 128)
    copies_1 = [
        send(sum_0.at[spots[k]], part_1.at[k], send_1, recv_1, k, rows_p[k])
        for k in range(1, plane_size)
    ]
    for copy in copies_1:
        copy.start()
    lax.fori_loop(0, 4, plane, 0)
    lax.fori_loop(0, 4, collect_far, 0)
    target = (beside[1], beside[0], beside[3], beside[2])
    returns = [send(far_out.at[d], far_in.at[d], ret_s, ret_r, d, target[d]) for d in range(4)]
    for copy in returns:
        copy.start()
    for copy in copies_1:
        copy.wait()
    result = sum_0[spot].astype(F32)
    for k in range(1, plane_size):
        result = result + part_1[k].astype(F32)
    part_2[z] = result.astype(BF16)
    copies_2 = [
        send(part_2.at[z], part_2.at[z], send_2, recv_2, k, rows_z[k - 1]) for k in range(1, nz)
    ]
    for copy in copies_2:
        copy.start()
    settle(octant_chunk)
    for k in range(8):
        coarse[k * 64 : k * 64 + 64, :] = merged_row(maps[0, k], octants, received)
    values = coarse[...].astype(F32)
    active = (values * sigmoid(values)).astype(BF16)
    latent_own[...] = dot(active, head[...], 1, 1).astype(BF16)
    lax.fori_loop(0, 4, collect_near, 0)
    for copy in returns:
        copy.wait()

    def store(i):
        return pltpu.make_async_copy(
            out_own.at[pl.ds(2 * i, 2)], out.at[pl.ds(2 * i, 2)], store_s.at[i]
        )

    def final(i, carry):
        cols = [hidden_grad[i, :, c * 128 : c * 128 + 128] for c in range(8)]
        for c in range(8):
            final_taps[0:64, c * 128 : c * 128 + 128] = cols[c]
        for d in range(6):
            face = near[d, i]
            if d < 4:
                face = face + far_in[d, i].astype(F32)
            moved = (shift_plus if d % 2 == 0 else shift_minus)(cols, d // 2, face.astype(BF16))
            for c in range(8):
                final_taps[64 * (d + 1) : 64 * (d + 2), c * 128 : c * 128 + 128] = moved[c]
        values = dot(turned[...], final_taps[...], 1, 0)
        keep_a = flag(counts[0] - 2 * i) > 0
        keep_b = flag(counts[0] - 2 * i) > 1
        for pq in range(4):
            even = values[:, pq * 256 : pq * 256 + 128]
            odd = values[:, pq * 256 + 128 : pq * 256 + 256]
            a = jnp.where(low_half, even, roll(odd, 64))
            b = jnp.where(low_half, roll(even, 64), odd)
            spread = slice(pq * 128, pq * 128 + 128)
            out_own[2 * i, :, spread] = jnp.where(keep_a, a, 0.0).astype(BF16)
            out_own[2 * i + 1, :, spread] = jnp.where(keep_b, b, 0.0).astype(BF16)
        return carry

    for copy in copies_2:
        copy.wait()
    result = part_2[0].astype(F32)
    for k in range(1, nz):
        result = result + part_2[k].astype(F32)
    part_3[spot] = result.astype(BF16)
    copies_3 = [
        send(part_3.at[spot], part_3.at[spot], send_3, recv_3, k, rows_p[k])
        for k in range(1, plane_size)
    ]
    for copy in copies_3:
        copy.start()
    lax.fori_loop(0, 4, final, 0)
    latent_store = pltpu.make_async_copy(latent_own, latent, store_s.at[4])
    latent_store.start()
    for i in range(4):
        store(i).start()
    for copy in copies_3:
        copy.wait()
    copy_4 = send(part_3, total.at[core], send_4, recv_4, 0, mate)
    copy_4.start()
    own_store = pltpu.make_async_copy(part_3, total.at[core], store_s.at[5])
    own_store.start()
    latent_store.wait()
    for i in range(4):
        store(i).wait()
    own_store.wait()
    copy_4.wait()


def unpack_kernel(
    latent, features, total, latent_out, features_out, conv_out, down_out, head_out,
    latent_hold, features_hold, total_hold, load_s, store_s,
):
    scale = float(2048) ** -0.5
    total_load = pltpu.make_async_copy(total, total_hold, load_s.at[0])
    latent_load = pltpu.make_async_copy(latent, latent_hold, load_s.at[1])
    features_load = pltpu.make_async_copy(features, features_hold, load_s.at[2])
    total_load.start()
    latent_load.start()
    features_load.start()
    latent_load.wait()
    latent_store = pltpu.make_async_copy(latent_hold, latent_out.at[0], store_s.at[0])
    latent_store.start()
    features_load.wait()
    features_store = pltpu.make_async_copy(features_hold, features_out, store_s.at[1])
    features_store.start()
    total_load.wait()
    rows = total_hold[...].reshape(GRAD_ROWS, 128).astype(F32) * scale
    for j in range(3):
        conv_out[:, j * 128 : j * 128 + 128] = rows[j * 64 : j * 64 + 64]
    conv_out[:, 384:448] = rows[192:256, :64]
    for j in range(4):
        down_out[:, j * 128 : j * 128 + 128] = rows[256 + j * 128 : 384 + j * 128]
    head_out[...] = rows[768:896]
    latent_store.wait()
    features_store.wait()


VM = pl.BlockSpec(memory_space=pltpu.VMEM)
SM = pl.BlockSpec(memory_space=pltpu.SMEM)
ANY = pl.BlockSpec(memory_space=pl.ANY)
DMA = pltpu.SemaphoreType.DMA
VMEM = pltpu.VMEM


def shape(*dims, dtype=BF16):
    return jax.ShapeDtypeStruct(dims, dtype)


def bind(kernel, *fixed):
    def run(*refs):
        kernel(*fixed, *refs)

    return run


def body(
    features, neighbours, counts, conv_weight, down_weight, head_weight, coarse_map, latent_grad
):
    n_gx, n_gy = lax.axis_size("gx"), lax.axis_size("gy")
    nz = ring_z(n_gx)
    spots = (n_gx // nz) * (n_gy // 2)
    per = GRAD_ROWS // 2 // spots
    pairs = [DMA((1,)), DMA((spots,)), DMA((nz,)), DMA((spots,)), DMA((1,))]
    latent, grad, total = pl.pallas_call(
        bind(step_kernel, n_gx, n_gy), name="step", in_specs=[SM] * 3 + [VM] * 3 + [ANY] * 2,
        out_specs=[ANY] * 3,
        out_shape=[shape(512, 128), shape(8, 64, 512), shape(2, spots, per, 128)],
        scratch_shapes=[
            VMEM((8, 64, 512), BF16), VMEM((8, 64, 128), BF16), VMEM((24, 64, 128), BF16),
            VMEM((6, 4, 64, 128), BF16), VMEM((4, 4, 64, 128), BF16),
            VMEM((8, 128), jnp.int32), VMEM((3, 8, 128), jnp.int32),
            VMEM((512, 128), BF16), VMEM((64, 448), BF16), VMEM((6, 2, 9, 64, 128), BF16),
            VMEM((4, 448, 1024), BF16), VMEM((4, 64, 1024), F32), VMEM((4, 512, 128), BF16),
            VMEM((8, 64, 128), BF16), VMEM((24, 64, 128), BF16),
            pltpu.SMEM((8,), jnp.int32), VMEM((4, 64, 1024), BF16), VMEM((6, 2, 4, 64, 128), F32),
            VMEM((6, 4, 64, 128), F32), VMEM((4, 4, 64, 128), BF16), VMEM((4, 4, 64, 128), BF16),
            VMEM((64, 448), F32), VMEM((512, 128), F32), VMEM((128, 128), F32),
            VMEM((448, 1024), BF16), VMEM((512, 128), BF16), VMEM((512, 128), BF16),
            VMEM((8, 64, 512), BF16),
            VMEM((2, 512, 128), BF16), VMEM((512, 128), BF16), VMEM((spots, per, 128), BF16),
            VMEM((spots, per, 128), BF16), VMEM((nz, per, 128), BF16), VMEM((spots, per, 128), BF16),
            DMA((5,)), DMA((6,)),
            DMA((7,)), DMA((7,)), DMA((12,)), DMA((12,)), DMA((12,)), DMA((12,)),
            DMA((4,)), DMA((4,)),
        ] + [pair for pair in pairs for _ in range(2)],
        compiler_params=pltpu.CompilerParams(collective_id=0, has_side_effects=True),
    )(
        counts, neighbours, coarse_map, conv_weight, down_weight, head_weight, features,
        latent_grad.reshape(8, 64, 128),
    )
    return pl.pallas_call(
        unpack_kernel, name="unpack", in_specs=[ANY] * 3, out_specs=[ANY] * 2 + [VM] * 3,
        out_shape=[
            shape(1, 512, 128), shape(8, 64, 512), shape(64, 448, dtype=F32),
            shape(128, 512, dtype=F32), shape(128, 128, dtype=F32),
        ],
        scratch_shapes=[
            VMEM((512, 128), BF16), VMEM((8, 64, 512), BF16), VMEM((2, spots, per, 128), BF16),
            DMA((3,)), DMA((2,)),
        ],
    )(latent, grad, total)


def solution(mesh):
    placed = (
        P(("gx", "gy"), None, None),
        P(("gx", "gy"), None),
        P(("gx", "gy")),
        P(),
        P(),
        P(),
        P(("gx", "gy"), None),
        P(("gx", "gy"), None, None),
    )
    return jax.shard_map(
        body,
        mesh=mesh,
        in_specs=placed,
        out_specs=(P(("gx", "gy"), None, None), P(("gx", "gy"), None, None), P(), P(), P()),
        check_vma=False,
    )
```

time: 59.5 us -> 47.2 us (0.79)
  Pallas kernels: 58 us -> 45.8 us
    pallas_call x1, Pallas kernels: 55.9 us -> 43 us  [body(): pl.pallas_call(bind(step_kernel, n_gx, n_gy), name='step', in_specs=[SM]...]
    pallas_call x1, Pallas kernels: 2.16 us -> 2.78 us  [body(): pl.pallas_call(unpack_kernel, name='unpack', in_specs=[ANY] * 3, out_spec...]
where the time goes in v3:
time: 47.2 us; the launch traced here: 47.1 us
  Pallas kernels  45.8 us (97%)
  between operations  1.29 us (3%)
    pallas_call x1, Pallas kernels, body(): pl.pallas_call(bind(step_kernel, n_gx, n_gy), name='step', in_specs=[SM]...  43 us
    pallas_call x1, Pallas kernels, body(): pl.pallas_call(unpack_kernel, name='unpack', in_specs=[ANY] * 3, out_spec...  2.78 us

profile of v3, /device:TPU:1, one launch (start us, length us, event | category | flops | bytes accessed | tf_op | source)
XLA Modules:
  0.0 47.1 jit_solution(16084188696478694591)
XLA Ops:
  1.3 43.0 %step.1 = (bf16[512,128]{1,0:T(8,128)(2,1)}, bf16[8,64,512]{2,1,0:T(8,128)(2,1)}, bf16[2,16,32,128]{3,2,1,0:T(8,128)(2,1)}) custom-call(s32[1]{0:T(128)S(6)} %copy.13.refs_0_, s32[8,6]{1,0:T(8,128)} %refs_1_.1, s32[1,8]{1,0:T(1,128)} %refs_2_.1, bf16[64,448]{1,0:T(8,128)(2,1)} %refs_3_.1, bf16[128,512]{1,0:T(8,128)(2,1)} %refs_4_.1, ...), custom_call_target="tpu_custom_call" | custom-call | tf_op jit(solution)/shard_map/step/pallas_call | solution.py:535
  44.3 2.8 %unpack.1 = (bf16[1,512,128]{2,1,0:T(8,128)(2,1)}, bf16[8,64,512]{2,1,0:T(8,128)(2,1)}, f32[64,448]{1,0:T(8,128)}, f32[128,512]{1,0:T(8,128)}, f32[128,128]{1,0:T(8,128)}) custom-call(bf16[512,128]{1,0:T(8,128)(2,1)} %get-tuple-element.8.latent, bf16[8,64,512]{2,1,0:T(8,128)(2,1)} %get-tuple-element.9.features, bf16[2,16,32,128]{3,2,1,0:T(8,128)(2,1)} %get-tuple-element.10.total), custom_call_target="tpu_custom_call" | custom-call | tf_op jit(solution)/shard_map/unpack/pallas_call | solution.py:562

commit v4 on v3

--- a/solution.py
+++ b/solution.py
@@ -122,13 +122,13 @@
 
 
 def step_kernel(
-    n_gx, n_gy, counts, links, maps, conv, down, head, features, grad_in,
+    n_gx, n_gy, counts, links, maps, conv_in, down_in, head_in, features, grad_in,
     latent, out, total,
-    blocks, grad_own, grad_far, faces, far, table, tables, down_rows, turned, pool, taps, hidden,
+    conv, down, head, blocks, grad_own, grad_far, table, tables, down_rows, turned, pool, tall, taps, hidden,
     act, octants, received, inverse, hidden_grad, planes, near, far_out, far_in, conv_acc, down_acc,
-    head_acc, final_taps, coarse, latent_own, out_own,
+    head_acc, final_taps, coarse,
     grads, part_0, sum_0, part_1, part_2, part_3,
-    load_s, store_s, face_s, face_r, merge_s, merge_r, back_s, back_r, ret_s, ret_r,
+    load_s, face_s, face_r, merge_s, merge_r, back_s, back_r, ret_s, ret_r,
     send_0, recv_0, send_1, recv_1, send_2, recv_2, send_3, recv_3, send_4, recv_4,
 ):
     nz = ring_z(n_gx)
@@ -172,13 +172,22 @@
         load(i).start()
     grad_load = pltpu.make_async_copy(grad_in, grad_own, load_s.at[4])
     grad_load.start()
+    weight_loads = [
+        pltpu.make_async_copy(source, target, load_s.at[5 + k])
+        for k, (source, target) in enumerate(((down_in, down), (conv_in, conv), (head_in, head)))
+    ]
+    for copy in weight_loads:
+        copy.start()
     lane = lax.broadcasted_iota(jnp.int32, (8, 128), 1)
     values = jnp.full((8, 128), -1, jnp.int32)
     for k in range(8):
         values = jnp.where(lane == k, jnp.broadcast_to(maps[0, k], (8, 128)), values)
     table[...] = values
-    down_rows[...] = dot(selection(), down[...], 1, 1).astype(BF16)
-
+    for d in range(4):
+        pool[d, 8] = zero
+    for d in range(2):
+        for j in range(4, 9):
+            tall[d, j] = zero
     def pack(i, carry):
         load(i).wait()
         keep_a = flag(counts[0] - 2 * i) > 0
@@ -190,16 +199,20 @@
             cols[2 * pq] = jnp.where(low_half, a, roll(b, 64))
             cols[2 * pq + 1] = jnp.where(low_half, roll(a, 64), b)
         for d in range(6):
-            faces[d, i] = pack_face(cols, d // 2, d % 2 == 0)
+            rows = pool.at[d, i] if d < 4 else tall.at[d - 4, i]
+            rows[...] = pack_face(cols, d // 2, d % 2 == 0)
         for c in range(8):
             taps[i, 0:64, c * 128 : c * 128 + 128] = cols[c]
         return carry
 
-    lax.fori_loop(0, 4, pack, 0)
+    lax.fori_loop(0, 4, pack, 0, unroll=True)
+    for copy in weight_loads:
+        copy.wait()
+    down_rows[...] = dot(selection(), down[...], 1, 1).astype(BF16)
     grad_load.wait()
     pl.semaphore_wait(barrier, len(everyone))
     face_copies = [
-        send(faces.at[d], far.at[d], face_s, face_r, d, beside[d]) for d in range(4)
+        send(pool.at[d, pl.ds(0, 4)], pool.at[d, pl.ds(4, 4)], face_s, face_r, d, beside[d]) for d in range(4)
     ] + [send(table, tables.at[m], face_s, face_r, 4 + m, merged[m]) for m in range(3)]
     for copy in face_copies:
         copy.start()
@@ -218,30 +231,15 @@
     for i in range(4):
         grad_chunk(i, 0).start()
         grad_chunk(i, 1).start()
-    for d in range(6):
-        pool[d, 0, 8] = zero
-        pool[d, 1, 8] = zero
-
-    def fill(j, carry):
-        for d in range(6):
-            own = faces[d, j]
-            pool[d, 0, j] = own
-            pool[d, 1, j] = roll(own, 64)
-            if d >= 4:
-                pool[d, 0, 4 + j] = zero
-                pool[d, 1, 4 + j] = zero
-        return carry
-
-    lax.fori_loop(0, 4, fill, 0)
-
     def tap(i, d):
         cols = [taps[i, 0:64, c * 128 : c * 128 + 128] for c in range(8)]
         e0 = link_of(links, 2 * i, d, rim)
         e1 = link_of(links, 2 * i + 1, d, rim)
+        rows = pool.at[d] if d < 4 else tall.at[d - 4]
         face = jnp.where(
             low_half,
-            pool[d, lax.rem(e0, 2), lax.div(e0, 2)],
-            pool[d, 1 - lax.rem(e1, 2), lax.div(e1, 2)],
+            pltpu.roll(rows[lax.div(e0, 2)], 64 * lax.rem(e0, 2), 1),
+            pltpu.roll(rows[lax.div(e1, 2)], 64 - 64 * lax.rem(e1, 2), 1),
         )
         moved = (shift_minus if d % 2 == 0 else shift_plus)(cols, d // 2, face)
         for c in range(8):
@@ -252,7 +250,7 @@
         tap(i, 5)
         return carry
 
-    lax.fori_loop(0, 4, upright, 0)
+    lax.fori_loop(0, 4, upright, 0, unroll=True)
     for d in range(7):
         block = conv[:, d * 64 : d * 64 + 64].astype(F32)
         turned[:, d * 64 : d * 64 + 64] = block.T.astype(BF16)
@@ -261,14 +259,6 @@
     head_acc[...] = jnp.zeros_like(head_acc)
     for copy in face_copies:
         copy.wait()
-
-    def fill_far(j, carry):
-        for d in range(4):
-            pool[d, 0, 4 + j] = far[d, j]
-            pool[d, 1, 4 + j] = roll(far[d, j], 64)
-        return carry
-
-    lax.fori_loop(0, 4, fill_far, 0)
 
     def level(i, carry):
         for d in range(4):
@@ -287,7 +277,7 @@
         grad_chunk(i, 2).start()
         return carry
 
-    lax.fori_loop(0, 4, level, 0)
+    lax.fori_loop(0, 4, level, 0, unroll=True)
     for s in range(8):
         found = jnp.zeros((8, 128), jnp.int32)
         for m in range(4):
@@ -331,7 +321,7 @@
         conv_acc[...] += dot(hidden_grad[i], taps[i], 1, 1)
         return carry
 
-    lax.fori_loop(0, 4, backward, 0)
+    lax.fori_loop(0, 4, backward, 0, unroll=True)
     wide = conv_acc[...].astype(BF16)
     for j in range(3):
         grads[0, j * 64 : j * 64 + 64, :] = wide[:, j * 128 : j * 128 + 128]
@@ -413,15 +403,10 @@
         coarse[k * 64 : k * 64 + 64, :] = merged_row(maps[0, k], octants, received)
     values = coarse[...].astype(F32)
     active = (values * sigmoid(values)).astype(BF16)
-    latent_own[...] = dot(active, head[...], 1, 1).astype(BF16)
+    latent[...] = dot(active, head[...], 1, 1).astype(BF16)
     lax.fori_loop(0, 4, collect_near, 0)
     for copy in returns:
         copy.wait()
-
-    def store(i):
-        return pltpu.make_async_copy(
-            out_own.at[pl.ds(2 * i, 2)], out.at[pl.ds(2 * i, 2)], store_s.at[i]
-        )
 
     def final(i, carry):
         cols = [hidden_grad[i, :, c * 128 : c * 128 + 128] for c in range(8)]
@@ -443,8 +428,8 @@
             a = jnp.where(low_half, even, roll(odd, 64))
             b = jnp.where(low_half, roll(even, 64), odd)
             spread = slice(pq * 128, pq * 128 + 128)
-            out_own[2 * i, :, spread] = jnp.where(keep_a, a, 0.0).astype(BF16)
-            out_own[2 * i + 1, :, spread] = jnp.where(keep_b, b, 0.0).astype(BF16)
+            out[2 * i, :, spread] = jnp.where(keep_a, a, 0.0).astype(BF16)
+            out[2 * i + 1, :, spread] = jnp.where(keep_b, b, 0.0).astype(BF16)
         return carry
 
     for copy in copies_2:
@@ -459,56 +444,50 @@
     ]
     for copy in copies_3:
         copy.start()
-    lax.fori_loop(0, 4, final, 0)
-    latent_store = pltpu.make_async_copy(latent_own, latent, store_s.at[4])
-    latent_store.start()
-    for i in range(4):
-        store(i).start()
+    lax.fori_loop(0, 4, final, 0, unroll=True)
     for copy in copies_3:
         copy.wait()
     copy_4 = send(part_3, total.at[core], send_4, recv_4, 0, mate)
     copy_4.start()
-    own_store = pltpu.make_async_copy(part_3, total.at[core], store_s.at[5])
-    own_store.start()
-    latent_store.wait()
-    for i in range(4):
-        store(i).wait()
-    own_store.wait()
+    total[core] = part_3[...]
     copy_4.wait()
 
 
 def unpack_kernel(
     latent, features, total, latent_out, features_out, conv_out, down_out, head_out,
-    latent_hold, features_hold, total_hold, load_s, store_s,
+    conv_hold, down_hold, head_hold, store_s,
 ):
     scale = float(2048) ** -0.5
-    total_load = pltpu.make_async_copy(total, total_hold, load_s.at[0])
-    latent_load = pltpu.make_async_copy(latent, latent_hold, load_s.at[1])
-    features_load = pltpu.make_async_copy(features, features_hold, load_s.at[2])
-    total_load.start()
-    latent_load.start()
-    features_load.start()
-    latent_load.wait()
-    latent_store = pltpu.make_async_copy(latent_hold, latent_out.at[0], store_s.at[0])
-    latent_store.start()
-    features_load.wait()
-    features_store = pltpu.make_async_copy(features_hold, features_out, store_s.at[1])
-    features_store.start()
-    total_load.wait()
-    rows = total_hold[...].reshape(GRAD_ROWS, 128).astype(F32) * scale
+    moves = [(features, features_out), (latent, latent_out.at[0])]
+    moves += [(conv_hold, conv_out), (down_hold, down_out), (head_hold, head_out)]
+    stores = [
+        pltpu.make_async_copy(source, target, store_s.at[k])
+        for k, (source, target) in enumerate(moves)
+    ]
+    stores[0].start()
+    stores[1].start()
+    rows = total[...].reshape(GRAD_ROWS, 128)
+
+    def scaled(first, last):
+        return rows[first:last].astype(F32) * scale
+
+    for j in range(4):
+        down_hold[:, j * 128 : j * 128 + 128] = scaled(256 + j * 128, 384 + j * 128)
+    stores[3].start()
     for j in range(3):
-        conv_out[:, j * 128 : j * 128 + 128] = rows[j * 64 : j * 64 + 64]
-    conv_out[:, 384:448] = rows[192:256, :64]
-    for j in range(4):
-        down_out[:, j * 128 : j * 128 + 128] = rows[256 + j * 128 : 384 + j * 128]
-    head_out[...] = rows[768:896]
-    latent_store.wait()
-    features_store.wait()
+        conv_hold[:, j * 128 : j * 128 + 128] = scaled(j * 64, j * 64 + 64)
+    conv_hold[:, 384:448] = scaled(192, 256)[:, :64]
+    stores[2].start()
+    head_hold[...] = scaled(768, 896)
+    stores[4].start()
+    for store in stores:
+        store.wait()
 
 
 VM = pl.BlockSpec(memory_space=pltpu.VMEM)
 SM = pl.BlockSpec(memory_space=pltpu.SMEM)
 ANY = pl.BlockSpec(memory_space=pl.ANY)
+HBM = pl.BlockSpec(memory_space=pltpu.HBM)
 DMA = pltpu.SemaphoreType.DMA
 VMEM = pltpu.VMEM
 
@@ -533,42 +512,48 @@
     per = GRAD_ROWS // 2 // spots
     pairs = [DMA((1,)), DMA((spots,)), DMA((nz,)), DMA((spots,)), DMA((1,))]
     latent, grad, total = pl.pallas_call(
-        bind(step_kernel, n_gx, n_gy), name="step", in_specs=[SM] * 3 + [VM] * 3 + [ANY] * 2,
-        out_specs=[ANY] * 3,
+        bind(step_kernel, n_gx, n_gy), name="step", in_specs=[SM] * 3 + [HBM] * 5,
+        out_specs=[VM] * 3,
         out_shape=[shape(512, 128), shape(8, 64, 512), shape(2, spots, per, 128)],
         scratch_shapes=[
+            VMEM((64, 448), BF16), VMEM((128, 512), BF16), VMEM((128, 128), BF16),
             VMEM((8, 64, 512), BF16), VMEM((8, 64, 128), BF16), VMEM((24, 64, 128), BF16),
-            VMEM((6, 4, 64, 128), BF16), VMEM((4, 4, 64, 128), BF16),
             VMEM((8, 128), jnp.int32), VMEM((3, 8, 128), jnp.int32),
-            VMEM((512, 128), BF16), VMEM((64, 448), BF16), VMEM((6, 2, 9, 64, 128), BF16),
+            VMEM((512, 128), BF16), VMEM((64, 448), BF16), VMEM((4, 9, 64, 128), BF16), VMEM((2, 9, 64, 128), BF16),
             VMEM((4, 448, 1024), BF16), VMEM((4, 64, 1024), F32), VMEM((4, 512, 128), BF16),
             VMEM((8, 64, 128), BF16), VMEM((24, 64, 128), BF16),
             pltpu.SMEM((8,), jnp.int32), VMEM((4, 64, 1024), BF16), VMEM((6, 2, 4, 64, 128), F32),
             VMEM((6, 4, 64, 128), F32), VMEM((4, 4, 64, 128), BF16), VMEM((4, 4, 64, 128), BF16),
             VMEM((64, 448), F32), VMEM((512, 128), F32), VMEM((128, 128), F32),
-            VMEM((448, 1024), BF16), VMEM((512, 128), BF16), VMEM((512, 128), BF16),
-            VMEM((8, 64, 512), BF16),
+            VMEM((448, 1024), BF16), VMEM((512, 128), BF16),
             VMEM((2, 512, 128), BF16), VMEM((512, 128), BF16), VMEM((spots, per, 128), BF16),
             VMEM((spots, per, 128), BF16), VMEM((nz, per, 128), BF16), VMEM((spots, per, 128), BF16),
-            DMA((5,)), DMA((6,)),
+            DMA((8,)),
             DMA((7,)), DMA((7,)), DMA((12,)), DMA((12,)), DMA((12,)), DMA((12,)),
             DMA((4,)), DMA((4,)),
         ] + [pair for pair in pairs for _ in range(2)],
-        compiler_params=pltpu.CompilerParams(collective_id=0, has_side_effects=True),
+        compiler_params=pltpu.CompilerParams(
+            collective_id=0, has_side_effects=True, vmem_limit_bytes=20 * 2**20
+        ),
     )(
-        counts, neighbours, coarse_map, conv_weight, down_weight, head_weight, features,
-        latent_grad.reshape(8, 64, 128),
+        counts, *[
+            pltpu.with_memory_space_constraint(value, pltpu.HBM)
+            for value in (
+                neighbours, coarse_map, conv_weight, down_weight, head_weight, features,
+                latent_grad.reshape(8, 64, 128),
+            )
+        ],
     )
     return pl.pallas_call(
-        unpack_kernel, name="unpack", in_specs=[ANY] * 3, out_specs=[ANY] * 2 + [VM] * 3,
+        unpack_kernel, name="unpack", in_specs=[VM] * 3, out_specs=[ANY] * 5,
         out_shape=[
             shape(1, 512, 128), shape(8, 64, 512), shape(64, 448, dtype=F32),
             shape(128, 512, dtype=F32), shape(128, 128, dtype=F32),
         ],
         scratch_shapes=[
-            VMEM((512, 128), BF16), VMEM((8, 64, 512), BF16), VMEM((2, spots, per, 128), BF16),
-            DMA((3,)), DMA((2,)),
+            VMEM((64, 448), F32), VMEM((128, 512), F32), VMEM((128, 128), F32), DMA((5,)),
         ],
+        compiler_params=pltpu.CompilerParams(vmem_limit_bytes=8 * 2**20),
     )(latent, grad, total)
 
 

time: 47.2 us -> 44.4 us (0.941)
  Pallas kernels: 45.8 us -> 43 us
    pallas_call x1, Pallas kernels: 2.78 us -> 1.02 us  [body(): pl.pallas_call(unpack_kernel, name='unpack', in_specs=[VM] * 3, out_specs...]
    pallas_call x1, Pallas kernels: 43 us -> 42 us  [body(): pl.pallas_call(bind(step_kernel, n_gx, n_gy), name='step', in_specs=[SM]...]
where the time goes in v4:
time: 44.4 us; the launch traced here: 44.3 us
  Pallas kernels  43 us (97%)
  between operations  1.29 us (3%)
    pallas_call x1, Pallas kernels, body(): pl.pallas_call(bind(step_kernel, n_gx, n_gy), name='step', in_specs=[SM]...  42 us
    pallas_call x1, Pallas kernels, body(): pl.pallas_call(unpack_kernel, name='unpack', in_specs=[VM] * 3, out_specs...  1.02 us

profile of v4, /device:TPU:1, one launch (start us, length us, event | category | flops | bytes accessed | tf_op | source)
XLA Modules:
  0.0 44.3 jit_solution(2438187962511865982)
XLA Ops:
  1.3 42.0 %step.1 = (bf16[512,128]{1,0:T(8,128)(2,1)S(1)}, bf16[8,64,512]{2,1,0:T(8,128)(2,1)S(1)}, bf16[2,16,32,128]{3,2,1,0:T(8,128)(2,1)S(1)}) custom-call(s32[1]{0:T(128)S(6)} %copy.13.refs_0_, s32[8,6]{1,0:T(8,128)} %refs_1_.1, s32[1,8]{1,0:T(1,128)} %refs_2_.1, bf16[64,448]{1,0:T(8,128)(2,1)} %refs_3_.1, bf16[128,512]{1,0:T(8,128)(2,1)} %refs_4_.1, ...), custom_call_target="tpu_custom_call" | custom-call | tf_op jit(solution)/shard_map/step/pallas_call | solution.py:514
  43.3 1.0 %unpack.1 = (bf16[1,512,128]{2,1,0:T(8,128)(2,1)}, bf16[8,64,512]{2,1,0:T(8,128)(2,1)}, f32[64,448]{1,0:T(8,128)}, f32[128,512]{1,0:T(8,128)}, f32[128,128]{1,0:T(8,128)}) custom-call(bf16[512,128]{1,0:T(8,128)(2,1)S(1)} %get-tuple-element.8.latent, bf16[8,64,512]{2,1,0:T(8,128)(2,1)S(1)} %get-tuple-element.9.features, ...), custom_call_target="tpu_custom_call" | custom-call | tf_op jit(solution)/shard_map/unpack/pallas_call | solution.py:547

commit v5 on v4

--- a/solution.py
+++ b/solution.py
@@ -81,11 +81,6 @@
     return 1.0 / (1.0 + jnp.exp(-values))
 
 
-def silu_grad(values):
-    s = sigmoid(values)
-    return s * (1.0 + values * (1.0 - s))
-
-
 def edges(n_gx, n_gy):
     x, y = lax.axis_index("gx"), lax.axis_index("gy")
     return (x == 0, x == n_gx - 1, y == 0, y == n_gy - 1)
@@ -124,11 +119,11 @@
 def step_kernel(
     n_gx, n_gy, counts, links, maps, conv_in, down_in, head_in, features, grad_in,
     latent, out, total,
-    conv, down, head, blocks, grad_own, grad_far, table, tables, down_rows, turned, pool, tall, taps, hidden,
+    conv, down, head, blocks, grad_own, grad_far, table, tables, down_rows, turned, pool, tall, taps, slope,
     act, octants, received, inverse, hidden_grad, planes, near, far_out, far_in, conv_acc, down_acc,
     head_acc, final_taps, coarse,
     grads, part_0, sum_0, part_1, part_2, part_3,
-    load_s, face_s, face_r, merge_s, merge_r, back_s, back_r, ret_s, ret_r,
+    known, load_s, face_s, face_r, merge_s, merge_r, back_s, back_r, ret_s, ret_r,
     send_0, recv_0, send_1, recv_1, send_2, recv_2, send_3, recv_3, send_4, recv_4,
 ):
     nz = ring_z(n_gx)
@@ -148,7 +143,20 @@
         other_y = lax.rem(y + k % ny, ny)
         rows_p.append((other_y * nz + z, other_c * 2 + core))
         spots.append(other_c * ny + other_y)
-    everyone = list(beside) + list(merged) + rows_z + rows_p[1:]
+    ring = [
+        (y * nz + lax.rem(z + 1, nz), me), (y * nz + lax.rem(z + nz - 1, nz), me),
+        (lax.rem(y + 1, ny) * nz + z, me), (lax.rem(y + ny - 1, ny) * nz + z, me),
+        (x, lax.rem(chip + 1, nc) * 2 + core), (x, lax.rem(chip + nc - 1, nc) * 2 + core),
+    ]
+    everyone = list(beside) + list(merged) + ring
+
+    def tell(number):
+        for device in ring:
+            pl.semaphore_signal(known.at[number], inc=1, device_id=device, device_id_type=MESH)
+
+    def hear(number):
+        pl.semaphore_wait(known.at[number], len(ring))
+
     rim = edges(n_gx, n_gy)
     low_half = lanes() < 64
     zero = jnp.zeros((64, 128), BF16)
@@ -211,6 +219,7 @@
     down_rows[...] = dot(selection(), down[...], 1, 1).astype(BF16)
     grad_load.wait()
     pl.semaphore_wait(barrier, len(everyone))
+    tell(0)
     face_copies = [
         send(pool.at[d, pl.ds(0, 4)], pool.at[d, pl.ds(4, 4)], face_s, face_r, d, beside[d]) for d in range(4)
     ] + [send(table, tables.at[m], face_s, face_r, 4 + m, merged[m]) for m in range(3)]
@@ -259,20 +268,21 @@
     head_acc[...] = jnp.zeros_like(head_acc)
     for copy in face_copies:
         copy.wait()
+    hear(0)
+    tell(1)
 
     def level(i, carry):
         for d in range(4):
             tap(i, d)
         values = dot(conv[...], taps[i], 1, 0)
-        hidden[i] = values
-        active = (values * sigmoid(values)).astype(BF16)
+        s = sigmoid(values)
+        slope[i] = s * (1.0 + values * (1.0 - s))
+        active = (values * s).astype(BF16)
         for c in range(8):
             act[i, c * 64 : c * 64 + 64, :] = active[:, c * 128 : c * 128 + 128]
         rows = dot(act[i], down_rows[...], 0, 0).astype(BF16)
         octants[2 * i] = rows[:64]
         octants[2 * i + 1] = rows[64:]
-        octant_chunk(i, 0).start()
-        octant_chunk(i, 1).start()
         grad_chunk(i, 0).wait_recv()
         grad_chunk(i, 2).start()
         return carry
@@ -294,6 +304,8 @@
 
         lax.fori_loop(0, 4, rest, 0)
 
+    hear(1)
+    tell(2)
     settle(grad_chunk)
 
     def merged_row(e, own, other):
@@ -315,8 +327,8 @@
         down_acc[...] += dot(act[i], rows, 1, 0)
         patch = dot(down_rows[...], rows, 1, 1)
         for c in range(8):
-            slope = silu_grad(hidden[i, :, c * 128 : c * 128 + 128])
-            value = (patch[c * 64 : c * 64 + 64] * slope).astype(BF16)
+            factor = slope[i, :, c * 128 : c * 128 + 128]
+            value = (patch[c * 64 : c * 64 + 64] * factor).astype(BF16)
             hidden_grad[i, :, c * 128 : c * 128 + 128] = value
         conv_acc[...] += dot(hidden_grad[i], taps[i], 1, 1)
         return carry
@@ -335,12 +347,9 @@
     copy_0 = send(grads.at[1 - core], part_0, send_0, recv_0, 0, mate)
     copy_0.start()
 
-    def relay(i, carry):
-        octant_chunk(i, 0).wait_recv()
-        octant_chunk(i, 2).start()
-        return carry
-
-    lax.fori_loop(0, 4, relay, 0)
+    for i in range(4):
+        octant_chunk(i, 0).start()
+        octant_chunk(i, 1).start()
 
     def plane(i, carry):
         cols = [hidden_grad[i, :, c * 128 : c * 128 + 128] for c in range(8)]
@@ -375,6 +384,7 @@
     result = grads[core].astype(F32) + part_0[...].astype(F32)
     per = result.shape[0] // plane_size
     sum_0[...] = result.astype(BF16).reshape(plane_size, per, 128)
+    hear(2)
     copies_1 = [
         send(sum_0.at[spots[k]], part_1.at[k], send_1, recv_1, k, rows_p[k])
         for k in range(1, plane_size)
@@ -398,12 +408,13 @@
     ]
     for copy in copies_2:
         copy.start()
-    settle(octant_chunk)
-    for k in range(8):
-        coarse[k * 64 : k * 64 + 64, :] = merged_row(maps[0, k], octants, received)
-    values = coarse[...].astype(F32)
-    active = (values * sigmoid(values)).astype(BF16)
-    latent[...] = dot(active, head[...], 1, 1).astype(BF16)
+    def relay(i, carry):
+        octant_chunk(i, 0).wait_recv()
+        octant_chunk(i, 2).start()
+        return carry
+
+    lax.fori_loop(0, 4, relay, 0)
+
     lax.fori_loop(0, 4, collect_near, 0)
     for copy in returns:
         copy.wait()
@@ -432,6 +443,7 @@
             out[2 * i + 1, :, spread] = jnp.where(keep_b, b, 0.0).astype(BF16)
         return carry
 
+    lax.fori_loop(0, 4, final, 0, unroll=True)
     for copy in copies_2:
         copy.wait()
     result = part_2[0].astype(F32)
@@ -444,13 +456,32 @@
     ]
     for copy in copies_3:
         copy.start()
-    lax.fori_loop(0, 4, final, 0, unroll=True)
+
+    def across(k):
+        origin = lax.rem(chip + nc - k // ny, nc) * ny + lax.rem(y + ny - k % ny, ny)
+        return send(part_3.at[origin], total.at[core, origin], send_4, recv_4, k, mate)
+
+    def hops(k):
+        return min(k // ny, nc - k // ny) + min(k % ny, ny - k % ny)
+
+    nearest = sorted(range(plane_size), key=hops)
+    copies_4 = [across(0)]
+    copies_4[0].start()
+    settle(octant_chunk)
+    for k in range(8):
+        coarse[k * 64 : k * 64 + 64, :] = merged_row(maps[0, k], octants, received)
+    values = coarse[...].astype(F32)
+    active = (values * sigmoid(values)).astype(BF16)
+    latent[...] = dot(active, head[...], 1, 1).astype(BF16)
+    for k in nearest[1:]:
+        copies_3[k - 1].wait_recv()
+        copies_4.append(across(k))
+        copies_4[-1].start()
     for copy in copies_3:
+        copy.wait_send()
+    total[core] = part_3[...]
+    for copy in copies_4:
         copy.wait()
-    copy_4 = send(part_3, total.at[core], send_4, recv_4, 0, mate)
-    copy_4.start()
-    total[core] = part_3[...]
-    copy_4.wait()
 
 
 def unpack_kernel(
@@ -510,7 +541,7 @@
     nz = ring_z(n_gx)
     spots = (n_gx // nz) * (n_gy // 2)
     per = GRAD_ROWS // 2 // spots
-    pairs = [DMA((1,)), DMA((spots,)), DMA((nz,)), DMA((spots,)), DMA((1,))]
+    pairs = [DMA((1,)), DMA((spots,)), DMA((nz,)), DMA((spots,)), DMA((spots,))]
     latent, grad, total = pl.pallas_call(
         bind(step_kernel, n_gx, n_gy), name="step", in_specs=[SM] * 3 + [HBM] * 5,
         out_specs=[VM] * 3,
@@ -528,7 +559,7 @@
             VMEM((448, 1024), BF16), VMEM((512, 128), BF16),
             VMEM((2, 512, 128), BF16), VMEM((512, 128), BF16), VMEM((spots, per, 128), BF16),
             VMEM((spots, per, 128), BF16), VMEM((nz, per, 128), BF16), VMEM((spots, per, 128), BF16),
-            DMA((8,)),
+            pltpu.SemaphoreType.REGULAR((3,)), DMA((8,)),
             DMA((7,)), DMA((7,)), DMA((12,)), DMA((12,)), DMA((12,)), DMA((12,)),
             DMA((4,)), DMA((4,)),
         ] + [pair for pair in pairs for _ in range(2)],

time: 44.4 us -> 42.8 us (0.964)
  Pallas kernels: 43 us -> 41.4 us
    pallas_call x1, Pallas kernels: 42 us -> 40.4 us  [body(): pl.pallas_call(bind(step_kernel, n_gx, n_gy), name='step', in_specs=[SM]...]
where the time goes in v5:
time: 42.8 us; the launch traced here: 42.7 us
  Pallas kernels  41.4 us (97%)
  between operations  1.29 us (3%)
    pallas_call x1, Pallas kernels, body(): pl.pallas_call(bind(step_kernel, n_gx, n_gy), name='step', in_specs=[SM]...  40.4 us
    pallas_call x1, Pallas kernels, body(): pl.pallas_call(unpack_kernel, name='unpack', in_specs=[VM] * 3, out_specs...  1.02 us

profile of v5, /device:TPU:1, one launch (start us, length us, event | category | flops | bytes accessed | tf_op | source)
XLA Modules:
  0.0 42.7 jit_solution(3096482187354420906)
XLA Ops:
  1.3 40.4 %step.1 = (bf16[512,128]{1,0:T(8,128)(2,1)S(1)}, bf16[8,64,512]{2,1,0:T(8,128)(2,1)S(1)}, bf16[2,16,32,128]{3,2,1,0:T(8,128)(2,1)S(1)}) custom-call(s32[1]{0:T(128)S(6)} %copy.13.refs_0_, s32[8,6]{1,0:T(8,128)} %refs_1_.1, s32[1,8]{1,0:T(1,128)} %refs_2_.1, bf16[64,448]{1,0:T(8,128)(2,1)} %refs_3_.1, bf16[128,512]{1,0:T(8,128)(2,1)} %refs_4_.1, ...), custom_call_target="tpu_custom_call" | custom-call | tf_op jit(solution)/shard_map/step/pallas_call | solution.py:545
  41.6 1.0 %unpack.1 = (bf16[1,512,128]{2,1,0:T(8,128)(2,1)}, bf16[8,64,512]{2,1,0:T(8,128)(2,1)}, f32[64,448]{1,0:T(8,128)}, f32[128,512]{1,0:T(8,128)}, f32[128,128]{1,0:T(8,128)}) custom-call(bf16[512,128]{1,0:T(8,128)(2,1)S(1)} %get-tuple-element.8.latent, bf16[8,64,512]{2,1,0:T(8,128)(2,1)S(1)} %get-tuple-element.9.features, ...), custom_call_target="tpu_custom_call" | custom-call | tf_op jit(solution)/shard_map/unpack/pallas_call | solution.py:578

commit v6 on v5

--- a/solution.py
+++ b/solution.py
@@ -117,14 +117,14 @@
 
 
 def step_kernel(
-    n_gx, n_gy, counts, links, maps, conv_in, down_in, head_in, features, grad_in,
+    n_gx, n_gy, counts, links_in, maps_in, conv_in, down_in, head_in, features, grad_in,
     latent, out, total,
-    conv, down, head, blocks, grad_own, grad_far, table, tables, down_rows, turned, pool, tall, taps, slope,
+    links, maps, conv, down, head, blocks, grad_own, grad_far, table, tables, down_rows, turned, pool, tall, taps, slope,
     act, octants, received, inverse, hidden_grad, planes, near, far_out, far_in, conv_acc, down_acc,
     head_acc, final_taps, coarse,
-    grads, part_0, sum_0, part_1, part_2, part_3,
+    grads, part_1, part_2, part_3,
     known, load_s, face_s, face_r, merge_s, merge_r, back_s, back_r, ret_s, ret_r,
-    send_0, recv_0, send_1, recv_1, send_2, recv_2, send_3, recv_3, send_4, recv_4,
+    send_1, recv_1, send_2, recv_2, send_3, recv_3,
 ):
     nz = ring_z(n_gx)
     ny, nc = n_gx // nz, n_gy // 2
@@ -137,16 +137,22 @@
     merged = partners()
     mate = merged[1]
     rows_z = [(y * nz + lax.rem(z + k, nz), me) for k in range(1, nz)]
-    rows_p, spots = [None], [None]
-    for k in range(1, plane_size):
-        other_c = lax.rem(chip + k // ny, nc)
-        other_y = lax.rem(y + k % ny, ny)
-        rows_p.append((other_y * nz + z, other_c * 2 + core))
-        spots.append(other_c * ny + other_y)
+    flat = []
+    for k in range(1, 2 * plane_size):
+        near_by = k % plane_size
+        across_c, across_y = near_by // ny, near_by % ny
+        other_c = lax.rem(chip + across_c, nc)
+        other_y = lax.rem(y + across_y, ny)
+        other = core if k < plane_size else 1 - core
+        far_off = min(across_c, nc - across_c) + min(across_y, ny - across_y)
+        device = (other_y * nz + z, other_c * 2 + other)
+        flat.append((far_off, k, device, other, other_c * ny + other_y))
+    flat.sort(key=lambda entry: -entry[0])
+    order_z = sorted(range(1, nz), key=lambda k: -min(k, nz - k))
     ring = [
         (y * nz + lax.rem(z + 1, nz), me), (y * nz + lax.rem(z + nz - 1, nz), me),
         (lax.rem(y + 1, ny) * nz + z, me), (lax.rem(y + ny - 1, ny) * nz + z, me),
-        (x, lax.rem(chip + 1, nc) * 2 + core), (x, lax.rem(chip + nc - 1, nc) * 2 + core),
+        (x, lax.rem(chip + 1, nc) * 2 + core), (x, lax.rem(chip + nc - 1, nc) * 2 + core), mate,
     ]
     everyone = list(beside) + list(merged) + ring
 
@@ -163,9 +169,12 @@
 
     def send(source, target, sends, recvs, k, device):
         return pltpu.make_async_remote_copy(
-            src_ref=source, dst_ref=target, send_sem=sends.at[k], recv_sem=recvs.at[k],
+            src_ref=source, dst_ref=target, send_sem=sends.at[k[0]], recv_sem=recvs.at[k[1]],
             device_id=device, device_id_type=MESH,
         )
+
+    def whole(like, sends, recvs, k):
+        return send(like, like, sends, recvs, k, mate)
 
     barrier = pltpu.get_barrier_semaphore()
     for device in everyone:
@@ -178,6 +187,12 @@
 
     for i in range(4):
         load(i).start()
+    table_loads = [
+        pltpu.make_async_copy(maps_in, maps, load_s.at[8]),
+        pltpu.make_async_copy(links_in, links, load_s.at[9]),
+    ]
+    for copy in table_loads:
+        copy.start()
     grad_load = pltpu.make_async_copy(grad_in, grad_own, load_s.at[4])
     grad_load.start()
     weight_loads = [
@@ -186,11 +201,6 @@
     ]
     for copy in weight_loads:
         copy.start()
-    lane = lax.broadcasted_iota(jnp.int32, (8, 128), 1)
-    values = jnp.full((8, 128), -1, jnp.int32)
-    for k in range(8):
-        values = jnp.where(lane == k, jnp.broadcast_to(maps[0, k], (8, 128)), values)
-    table[...] = values
     for d in range(4):
         pool[d, 8] = zero
     for d in range(2):
@@ -214,6 +224,13 @@
         return carry
 
     lax.fori_loop(0, 4, pack, 0, unroll=True)
+    for copy in table_loads:
+        copy.wait()
+    lane = lax.broadcasted_iota(jnp.int32, (8, 128), 1)
+    values = jnp.full((8, 128), -1, jnp.int32)
+    for k in range(8):
+        values = jnp.where(lane == k, jnp.broadcast_to(maps[0, k], (8, 128)), values)
+    table[...] = values
     for copy in weight_loads:
         copy.wait()
     down_rows[...] = dot(selection(), down[...], 1, 1).astype(BF16)
@@ -221,25 +238,34 @@
     pl.semaphore_wait(barrier, len(everyone))
     tell(0)
     face_copies = [
-        send(pool.at[d, pl.ds(0, 4)], pool.at[d, pl.ds(4, 4)], face_s, face_r, d, beside[d]) for d in range(4)
-    ] + [send(table, tables.at[m], face_s, face_r, 4 + m, merged[m]) for m in range(3)]
+        send(pool.at[d, pl.ds(0, 4)], pool.at[d, pl.ds(4, 4)], face_s, face_r, (0, 0), beside[d])
+        for d in range(4)
+    ] + [send(table, tables.at[m], face_s, face_r, (1, 1), merged[m]) for m in range(3)]
     for copy in face_copies:
         copy.start()
 
-    def chunk(source, target, sends, recvs, i, leg):
-        rows = (source if leg < 2 else target).at[pl.ds(2 * i, 2)]
-        place = target.at[pl.ds(8 * leg + 2 * i, 2)]
-        return send(rows, place, sends, recvs, 4 * leg + i, merged[0] if leg == 0 else mate)
-
-    def grad_chunk(i, leg):
-        return chunk(grad_own, grad_far, back_s, back_r, i, leg)
-
-    def octant_chunk(i, leg):
-        return chunk(octants, received, merge_s, merge_r, i, leg)
-
+    def grad_chunk(i):
+        return send(
+            grad_own.at[pl.ds(2 * i, 2)], grad_far.at[pl.ds(2 * i, 2)], back_s, back_r,
+            (0, i), merged[0],
+        )
+
+    def grad_relay(i):
+        return send(
+            grad_far.at[pl.ds(2 * i, 2)], grad_far.at[pl.ds(16 + 2 * i, 2)], back_s, back_r,
+            (2, 5), mate,
+        )
+
+    grad_mate = send(grad_own, grad_far.at[pl.ds(8, 8)], back_s, back_r, (1, 4), mate)
+    octant_far = send(octants, received.at[pl.ds(0, 8)], merge_s, merge_r, (0, 0), merged[0])
+    octant_mate = send(octants, received.at[pl.ds(8, 8)], merge_s, merge_r, (1, 1), mate)
+    octant_relay = send(
+        received.at[pl.ds(0, 8)], received.at[pl.ds(16, 8)], merge_s, merge_r, (2, 2), mate
+    )
     for i in range(4):
-        grad_chunk(i, 0).start()
-        grad_chunk(i, 1).start()
+        grad_chunk(i).start()
+    grad_mate.start()
+
     def tap(i, d):
         cols = [taps[i, 0:64, c * 128 : c * 128 + 128] for c in range(8)]
         e0 = link_of(links, 2 * i, d, rim)
@@ -266,8 +292,8 @@
     conv_acc[...] = jnp.zeros_like(conv_acc)
     down_acc[...] = jnp.zeros_like(down_acc)
     head_acc[...] = jnp.zeros_like(head_acc)
-    for copy in face_copies:
-        copy.wait()
+    whole(far_in, face_s, face_r, (0, 0)).wait()
+    whole(tables, face_s, face_r, (1, 1)).wait()
     hear(0)
     tell(1)
 
@@ -283,8 +309,8 @@
         rows = dot(act[i], down_rows[...], 0, 0).astype(BF16)
         octants[2 * i] = rows[:64]
         octants[2 * i + 1] = rows[64:]
-        grad_chunk(i, 0).wait_recv()
-        grad_chunk(i, 2).start()
+        grad_chunk(i).wait_recv()
+        grad_relay(i).start()
         return carry
 
     lax.fori_loop(0, 4, level, 0, unroll=True)
@@ -295,18 +321,11 @@
             found = jnp.where(entries == m * 8 + s, m * 8 + lane - 32, found)
         inverse[s] = jnp.clip(jnp.sum(found[0:1, :]) + 32, 0, 32)
 
-    def settle(part):
-        def rest(i, carry):
-            part(i, 0).wait_send()
-            part(i, 1).wait()
-            part(i, 2).wait()
-            return carry
-
-        lax.fori_loop(0, 4, rest, 0)
-
     hear(1)
     tell(2)
-    settle(grad_chunk)
+    whole(grad_own, back_s, back_r, (0, 0)).wait_send()
+    grad_mate.wait()
+    whole(grad_own, back_s, back_r, (2, 5)).wait()
 
     def merged_row(e, own, other):
         mine = own[jnp.clip(e, 0, 7)]
@@ -334,22 +353,32 @@
         return carry
 
     lax.fori_loop(0, 4, backward, 0, unroll=True)
+    per = GRAD_ROWS // 2 // plane_size
+
+    def put(row, values):
+        half, first = row // (GRAD_ROWS // 2), row % (GRAD_ROWS // 2) // per
+        count = values.shape[0] // per
+        grads[half, first : first + count] = values.reshape(count, per, 128)
+
     wide = conv_acc[...].astype(BF16)
     for j in range(3):
-        grads[0, j * 64 : j * 64 + 64, :] = wide[:, j * 128 : j * 128 + 128]
-    grads[0, 192:256, :] = jnp.concatenate([wide[:, 384:448], jnp.zeros((64, 64), BF16)], axis=1)
+        put(j * 64, wide[:, j * 128 : j * 128 + 128])
+    put(192, jnp.concatenate([wide[:, 384:448], jnp.zeros((64, 64), BF16)], axis=1))
     ordered = dot(down_acc[...].astype(BF16), selection(), 0, 0).astype(BF16)
     for j in range(4):
-        row = 256 + 128 * (j % 2) if j < 2 else 128 * (j % 2)
-        grads[j // 2, row : row + 128, :] = ordered[:, j * 128 : j * 128 + 128]
-    grads[1, 256:384, :] = head_acc[...].astype(BF16)
-    grads[1, 384:512, :] = jnp.zeros((128, 128), BF16)
-    copy_0 = send(grads.at[1 - core], part_0, send_0, recv_0, 0, mate)
-    copy_0.start()
-
-    for i in range(4):
-        octant_chunk(i, 0).start()
-        octant_chunk(i, 1).start()
+        put(256 + 128 * j, ordered[:, j * 128 : j * 128 + 128])
+    put(768, head_acc[...].astype(BF16))
+    put(896, jnp.zeros((128, 128), BF16))
+    hear(2)
+    tell(3)
+    copies_1 = [
+        send(grads.at[half, place], part_1.at[k], send_1, recv_1, (0, 0), device)
+        for _, k, device, half, place in flat
+    ]
+    for copy in copies_1:
+        copy.start()
+    octant_far.start()
+    octant_mate.start()
 
     def plane(i, carry):
         cols = [hidden_grad[i, :, c * 128 : c * 128 + 128] for c in range(8)]
@@ -380,44 +409,27 @@
             near[d, j] = gathered(d, j)
         return carry
 
-    copy_0.wait()
-    result = grads[core].astype(F32) + part_0[...].astype(F32)
-    per = result.shape[0] // plane_size
-    sum_0[...] = result.astype(BF16).reshape(plane_size, per, 128)
-    hear(2)
-    copies_1 = [
-        send(sum_0.at[spots[k]], part_1.at[k], send_1, recv_1, k, rows_p[k])
-        for k in range(1, plane_size)
-    ]
-    for copy in copies_1:
-        copy.start()
     lax.fori_loop(0, 4, plane, 0)
     lax.fori_loop(0, 4, collect_far, 0)
     target = (beside[1], beside[0], beside[3], beside[2])
-    returns = [send(far_out.at[d], far_in.at[d], ret_s, ret_r, d, target[d]) for d in range(4)]
+    returns = [send(far_out.at[d], far_in.at[d], ret_s, ret_r, (0, 0), target[d]) for d in range(4)]
     for copy in returns:
         copy.start()
-    for copy in copies_1:
-        copy.wait()
-    result = sum_0[spot].astype(F32)
-    for k in range(1, plane_size):
+    others = part_1.at[pl.ds(1, 2 * plane_size - 1)]
+    whole(others, send_1, recv_1, (0, 0)).wait()
+    result = grads[core, spot].astype(F32)
+    for k in range(1, 2 * plane_size):
         result = result + part_1[k].astype(F32)
     part_2[z] = result.astype(BF16)
     copies_2 = [
-        send(part_2.at[z], part_2.at[z], send_2, recv_2, k, rows_z[k - 1]) for k in range(1, nz)
+        send(part_2.at[z], part_2.at[z], send_2, recv_2, (0, 0), rows_z[k - 1]) for k in order_z
     ]
     for copy in copies_2:
         copy.start()
-    def relay(i, carry):
-        octant_chunk(i, 0).wait_recv()
-        octant_chunk(i, 2).start()
-        return carry
-
-    lax.fori_loop(0, 4, relay, 0)
-
+    octant_far.wait_recv()
+    octant_relay.start()
     lax.fori_loop(0, 4, collect_near, 0)
-    for copy in returns:
-        copy.wait()
+    whole(far_in, ret_s, ret_r, (0, 0)).wait()
 
     def final(i, carry):
         cols = [hidden_grad[i, :, c * 128 : c * 128 + 128] for c in range(8)]
@@ -444,44 +456,28 @@
         return carry
 
     lax.fori_loop(0, 4, final, 0, unroll=True)
-    for copy in copies_2:
-        copy.wait()
+    whole(part_2.at[pl.ds(0, nz - 1)], send_2, recv_2, (0, 0)).wait()
     result = part_2[0].astype(F32)
     for k in range(1, nz):
         result = result + part_2[k].astype(F32)
-    part_3[spot] = result.astype(BF16)
+    part_3[...] = result.astype(BF16)
+    hear(3)
     copies_3 = [
-        send(part_3.at[spot], part_3.at[spot], send_3, recv_3, k, rows_p[k])
-        for k in range(1, plane_size)
+        send(part_3, total.at[core, spot], send_3, recv_3, (0, 0), device)
+        for _, _, device, _, _ in flat
     ]
     for copy in copies_3:
         copy.start()
-
-    def across(k):
-        origin = lax.rem(chip + nc - k // ny, nc) * ny + lax.rem(y + ny - k % ny, ny)
-        return send(part_3.at[origin], total.at[core, origin], send_4, recv_4, k, mate)
-
-    def hops(k):
-        return min(k // ny, nc - k // ny) + min(k % ny, ny - k % ny)
-
-    nearest = sorted(range(plane_size), key=hops)
-    copies_4 = [across(0)]
-    copies_4[0].start()
-    settle(octant_chunk)
+    total[core, spot] = result.astype(BF16)
+    octant_far.wait_send()
+    octant_mate.wait()
+    octant_relay.wait()
     for k in range(8):
         coarse[k * 64 : k * 64 + 64, :] = merged_row(maps[0, k], octants, received)
     values = coarse[...].astype(F32)
     active = (values * sigmoid(values)).astype(BF16)
     latent[...] = dot(active, head[...], 1, 1).astype(BF16)
-    for k in nearest[1:]:
-        copies_3[k - 1].wait_recv()
-        copies_4.append(across(k))
-        copies_4[-1].start()
-    for copy in copies_3:
-        copy.wait_send()
-    total[core] = part_3[...]
-    for copy in copies_4:
-        copy.wait()
+    whole(others, send_3, recv_3, (0, 0)).wait()
 
 
 def unpack_kernel(
@@ -541,12 +537,12 @@
     nz = ring_z(n_gx)
     spots = (n_gx // nz) * (n_gy // 2)
     per = GRAD_ROWS // 2 // spots
-    pairs = [DMA((1,)), DMA((spots,)), DMA((nz,)), DMA((spots,)), DMA((spots,))]
     latent, grad, total = pl.pallas_call(
-        bind(step_kernel, n_gx, n_gy), name="step", in_specs=[SM] * 3 + [HBM] * 5,
+        bind(step_kernel, n_gx, n_gy), name="step", in_specs=[SM] + [HBM] * 7,
         out_specs=[VM] * 3,
         out_shape=[shape(512, 128), shape(8, 64, 512), shape(2, spots, per, 128)],
         scratch_shapes=[
+            pltpu.SMEM((8, 6), jnp.int32), pltpu.SMEM((1, 8), jnp.int32),
             VMEM((64, 448), BF16), VMEM((128, 512), BF16), VMEM((128, 128), BF16),
             VMEM((8, 64, 512), BF16), VMEM((8, 64, 128), BF16), VMEM((24, 64, 128), BF16),
             VMEM((8, 128), jnp.int32), VMEM((3, 8, 128), jnp.int32),
@@ -557,12 +553,12 @@
             VMEM((6, 4, 64, 128), F32), VMEM((4, 4, 64, 128), BF16), VMEM((4, 4, 64, 128), BF16),
             VMEM((64, 448), F32), VMEM((512, 128), F32), VMEM((128, 128), F32),
             VMEM((448, 1024), BF16), VMEM((512, 128), BF16),
-            VMEM((2, 512, 128), BF16), VMEM((512, 128), BF16), VMEM((spots, per, 128), BF16),
-            VMEM((spots, per, 128), BF16), VMEM((nz, per, 128), BF16), VMEM((spots, per, 128), BF16),
-            pltpu.SemaphoreType.REGULAR((3,)), DMA((8,)),
-            DMA((7,)), DMA((7,)), DMA((12,)), DMA((12,)), DMA((12,)), DMA((12,)),
-            DMA((4,)), DMA((4,)),
-        ] + [pair for pair in pairs for _ in range(2)],
+            VMEM((2, spots, per, 128), BF16), VMEM((2 * spots, per, 128), BF16),
+            VMEM((nz, per, 128), BF16), VMEM((per, 128), BF16),
+            pltpu.SemaphoreType.REGULAR((4,)), DMA((10,)),
+            DMA((2,)), DMA((2,)), DMA((3,)), DMA((3,)), DMA((3,)), DMA((6,)),
+            DMA((1,)), DMA((1,)), DMA((1,)), DMA((1,)), DMA((1,)), DMA((1,)), DMA((1,)), DMA((1,)),
+        ],
         compiler_params=pltpu.CompilerParams(
             collective_id=0, has_side_effects=True, vmem_limit_bytes=20 * 2**20
         ),

time: 42.8 us -> 39.7 us (0.928)
  Pallas kernels: 41.4 us -> 38.3 us
    pallas_call x1, Pallas kernels: 40.4 us -> 37.3 us  [body(): pl.pallas_call(bind(step_kernel, n_gx, n_gy), name='step', in_specs=[SM]...]
where the time goes in v6:
time: 39.7 us; the launch traced here: 39.6 us
  Pallas kernels  38.3 us (96%)
  between operations  1.29 us (3%)
    pallas_call x1, Pallas kernels, body(): pl.pallas_call(bind(step_kernel, n_gx, n_gy), name='step', in_specs=[SM]...  37.3 us
    pallas_call x1, Pallas kernels, body(): pl.pallas_call(unpack_kernel, name='unpack', in_specs=[VM] * 3, out_specs...  1.02 us

profile of v6, /device:TPU:1, one launch (start us, length us, event | category | flops | bytes accessed | tf_op | source)
XLA Modules:
  0.0 39.6 jit_solution(11787417265258415820)
XLA Ops:
  1.3 37.3 %step.1 = (bf16[512,128]{1,0:T(8,128)(2,1)S(1)}, bf16[8,64,512]{2,1,0:T(8,128)(2,1)S(1)}, bf16[2,16,32,128]{3,2,1,0:T(8,128)(2,1)S(1)}) custom-call(s32[1]{0:T(128)S(6)} %copy.13.refs_0_, s32[8,6]{1,0:T(8,128)} %refs_1_.1, s32[1,8]{1,0:T(1,128)} %refs_2_.1, bf16[64,448]{1,0:T(8,128)(2,1)} %refs_3_.1, bf16[128,512]{1,0:T(8,128)(2,1)} %refs_4_.1, ...), custom_call_target="tpu_custom_call" | custom-call | tf_op jit(solution)/shard_map/step/pallas_call | solution.py:540
  38.6 1.0 %unpack.1 = (bf16[1,512,128]{2,1,0:T(8,128)(2,1)}, bf16[8,64,512]{2,1,0:T(8,128)(2,1)}, f32[64,448]{1,0:T(8,128)}, f32[128,512]{1,0:T(8,128)}, f32[128,128]{1,0:T(8,128)}) custom-call(bf16[512,128]{1,0:T(8,128)(2,1)S(1)} %get-tuple-element.8.latent, bf16[8,64,512]{2,1,0:T(8,128)(2,1)S(1)} %get-tuple-element.9.features, ...), custom_call_target="tpu_custom_call" | custom-call | tf_op jit(solution)/shard_map/unpack/pallas_call | solution.py:574
